TPU v7x, 256 devices: a whole 4x4x8 slice. The times are simulated.
256 devices in a mesh: dp: 16 (over y, x_lo, core), seq: 16 (over z, x_hi).
Axes of the slice: x: 4 (x_hi: 2, x_lo: 2; x = x_hi * 2 + x_lo), y: 4, z: 8, core: 2. Of those that a mesh axis runs over, the one named last changes fastest.
Arguments:
- queries: bfloat16 [131072, 1536], P(('dp', 'seq')), may hold values from -8 to 8
- keys: bfloat16 [131072, 1536], P(('dp', 'seq')), may hold values from -8 to 8
- values: bfloat16 [131072, 1536], P(('dp', 'seq')), may hold values from -6 to 6
- grad_out: bfloat16 [131072, 1536], P(('dp', 'seq')), may hold values from -24 to 24
- out_weight: bfloat16 [1536, 1536], P('dp'), may hold values from -0.15625 to 0.15625
- lengths: int32 [16], P('dp'), may hold values from 1024 to 8192, as said below
Outputs:
- grad_queries: bfloat16 [131072, 1536], P(('dp', 'seq'))
- grad_keys: bfloat16 [131072, 1536], P(('dp', 'seq'))
- grad_values: bfloat16 [131072, 1536], P(('dp', 'seq'))
- grad_weight: float32 [1536, 1536], P(('dp', 'seq'))
Inputs may be any that keep to these rules, and one draw needn't show every extreme that they name: `lengths`: every draw holds one stretch of 8192 valid bytes and one of 1024.
All inputs are finite; a program needn't handle non-finite values.
Results may differ from a plain program's by a relative error of at most 0.0058.
Values may be sent and summed in bfloat16 or wider, within the bound.
No kernel may reach another device: no remote copies, remote signals or barrier semaphores. Data moves between devices by JAX's collectives and lax.ppermute only.
A program may use at most 192 MiB of HBM per device.

v0:
```python
import jax
import jax.numpy as jnp
from jax import lax
from jax.sharding import PartitionSpec as P

HEADS = 12
HEAD_DIM = 128
WINDOW = 512


def extended(block, sides, width):
    for axis, dim in sides:
        count = lax.axis_size(axis)
        forward = [(i, i + 1) for i in range(count - 1)]
        backward = [(target, source) for source, target in forward]
        low = lax.ppermute(
            lax.slice_in_dim(block, block.shape[dim] - width, None, axis=dim), axis, forward
        )
        high = lax.ppermute(lax.slice_in_dim(block, 0, width, axis=dim), axis, backward)
        block = jnp.concatenate([low, block, high], axis=dim)
    return block


def passed_along(value, axis, by):
    devices = lax.axis_size(axis)
    pairs = [(i, i + by) for i in range(devices) if 0 <= i + by < devices]
    return lax.ppermute(value, axis, pairs)


def window_backward(query_block, key_window, value_window, grad_block, query_pos, key_pos, length):
    half_window = WINDOW // 2
    inv_root = HEAD_DIM ** (-0.5)
    offset = key_pos[None, :] - query_pos[:, None]
    allowed = (offset >= -half_window) & (offset < half_window)
    allowed = (
        allowed
        & (key_pos[None, :] >= 0)
        & (key_pos[None, :] < length)
        & (query_pos[:, None] < length)
    )

    def split_heads(matrix):
        return matrix.reshape(matrix.shape[0], HEADS, HEAD_DIM).transpose(1, 0, 2)

    def join_heads(stacked):
        return stacked.transpose(1, 0, 2).reshape(stacked.shape[1], HEADS * HEAD_DIM)

    def one_head(operands):
        query_head, key_head, value_head, grad_head = operands
        scores = (
            lax.dot_general(
                query_head, key_head, (((1,), (1,)), ((), ())), preferred_element_type=jnp.float32
            )
            * inv_root
        )
        scores = jnp.where(allowed, scores, -1e30)
        row_max = jnp.max(scores, axis=1, keepdims=True)
        expo = jnp.where(allowed, jnp.exp(scores - row_max), 0.0)
        row_total = jnp.maximum(jnp.sum(expo, axis=1, keepdims=True), 1.0)
        probability = expo / row_total
        probability_b = probability.astype(jnp.bfloat16)
        attended_head = jnp.dot(probability_b, value_head, preferred_element_type=jnp.float32)
        grad_probs = lax.dot_general(
            grad_head, value_head, (((1,), (1,)), ((), ())), preferred_element_type=jnp.float32
        )
        row_delta = jnp.sum(probability * grad_probs, axis=1, keepdims=True)
        grad_scores = (probability * (grad_probs - row_delta) * inv_root).astype(jnp.bfloat16)
        grad_query = jnp.dot(grad_scores, key_head, preferred_element_type=jnp.float32)
        grad_key = lax.dot_general(
            grad_scores, query_head, (((0,), (0,)), ((), ())), preferred_element_type=jnp.float32
        )
        grad_value = lax.dot_general(
            probability_b, grad_head, (((0,), (0,)), ((), ())), preferred_element_type=jnp.float32
        )
        return (attended_head, grad_query, grad_key, grad_value)

    outputs = lax.map(
        one_head,
        (
            split_heads(query_block),
            split_heads(key_window),
            split_heads(value_window),
            split_heads(grad_block),
        ),
    )
    attended_heads, grad_query, grad_key, grad_value = outputs
    return (
        join_heads(attended_heads).astype(jnp.bfloat16),
        join_heads(grad_query),
        join_heads(grad_key),
        join_heads(grad_value),
    )


def shards(queries, keys, values, grad_out, out_weight, lengths):
    tok_rows, feat_width = queries.shape
    half_window = WINDOW // 2
    window_rows = tok_rows + 2 * half_window
    seq_index = lax.axis_index("seq")
    first_row = seq_index * tok_rows
    length = lengths[0]
    grad_mixed = jnp.dot(
        grad_out,
        lax.all_gather(out_weight, "dp", axis=0, tiled=True),
        preferred_element_type=jnp.float32,
    ).astype(jnp.bfloat16)
    stacked = jnp.stack([keys, values])
    padded = extended(stacked, (("seq", 1),), half_window)
    query_pos = first_row + jnp.arange(tok_rows, dtype=jnp.int32)
    key_pos = first_row - half_window + jnp.arange(window_rows, dtype=jnp.int32)
    attended, grad_query, grad_key, grad_value = window_backward(
        queries, padded[0], padded[1], grad_mixed, query_pos, key_pos, length
    )
    rim_grads = jnp.stack([grad_key, grad_value])
    from_right = passed_along(rim_grads[:, :half_window], "seq", -1)
    from_left = passed_along(rim_grads[:, tok_rows + half_window :], "seq", 1)
    own_grads = rim_grads[:, half_window : half_window + tok_rows]
    own_grads = own_grads.at[:, :half_window].add(from_left)
    own_grads = own_grads.at[:, tok_rows - half_window :].add(from_right)
    weight_grad = lax.psum_scatter(
        lax.dot_general(
            grad_out, attended, (((0,), (0,)), ((), ())), preferred_element_type=jnp.float32
        ),
        ("dp", "seq"),
        scatter_dimension=0,
        tiled=True,
    )
    return (
        grad_query.astype(jnp.bfloat16),
        own_grads[0].astype(jnp.bfloat16),
        own_grads[1].astype(jnp.bfloat16),
        weight_grad,
    )


def solution(mesh):
    in_specs = (
        P(("dp", "seq"), None),
        P(("dp", "seq"), None),
        P(("dp", "seq"), None),
        P(("dp", "seq"), None),
        P("dp", None),
        P("dp"),
    )
    out_specs = (
        P(("dp", "seq"), None),
        P(("dp", "seq"), None),
        P(("dp", "seq"), None),
        P(("dp", "seq"), None),
    )
    return jax.shard_map(shards, mesh=mesh, in_specs=in_specs, out_specs=out_specs, check_vma=False)
```

profile of v0, /device:TPU:18, one launch (start us, length us, event | category | flops | bytes accessed | tf_op | source)
XLA Modules:
  0.0 729.8 jit_solution(2500829251480583825)
XLA Ops:
  15.5 5.3 collective-permute-start
  25.4 61.8 %collective-permute-done = bf16[2,256,1536]{1,2,0:T(8,128)(2,1)} collective-permute-done((bf16[2,256,1536]{1,2,0:T(8,128)(2,1)}, bf16[2,256,1536]{1,2,0:T(8,128)(2,1)}, u32[]{:S(2)}, u32[]{:S(2)}) %collective-permute-start) | collective-permute-done | bytes 1572896 | tf_op jit(solution)/shard_map/ppermute | solution.py:16
  87.2 3.3 pad_maximum_fusion
  90.5 3.5 fusion.50
  94.1 8.0 %all-gather.2.cloned.1.call-done = bf16[1536,1536]{1,0:T(8,128)(2,1)} async-done(((bf16[96,1536]{1,0:T(8,128)(2,1)}), bf16[1536,1536]{1,0:T(8,128)(2,1)}) %all-gather.2.cloned.1.call-update) | async-done | bytes 4718608 | tf_op jit(solution)/shard_map/all_gather | solution.py:104
  102.1 6.0 convolution_convert_fusion
  109.8 210.1 %while.19 = (s32[]{:T(128)}, bf16[12,512,128]{1,2,0:T(8,128)(2,1)}, bf16[12,512,128]{1,2,0:T(8,128)(2,1)}, f32[12,1024,128]{1,2,0:T(8,128)}, f32[12,1024,128]{1,...) while((s32[]{:T(128)}, bf16[12,512,128]{1,2,0:T(8,128)(2,1)}, ...), condition=%wide.region_4.5_spmd.clone, body=%wide.region_0.4_spmd.clone.sunk | while | flops 846199808 | bytes 23157900 | solution.py:77
  124.0 3.3 fusion.81
  141.6 3.3 fusion.81
  159.1 3.3 fusion.81
  176.5 3.3 fusion.81
  194.1 3.3 fusion.81
  211.5 3.3 fusion.81
  229.1 3.3 fusion.81
  264.1 3.3 fusion.81
  281.6 3.3 fusion.81
  299.1 3.3 fusion.81
  319.9 3.8 fusion.42
  326.6 6.4 convolution_bitcast_fusion.4
  333.1 6.3 fusion.41
  339.4 61.8 %collective-permute-done.2 = f32[2,256,1536]{1,2,0:T(8,128)} collective-permute-done((f32[2,256,1536]{1,2,0:T(8,128)}, f32[2,256,1536]{1,2,0:T(8,128)}, u32[]{:S(2)}, u32[]{:S(2)}) %collective-permute-start.2) | collective-permute-done | bytes 3145760 | tf_op jit(solution)/shard_map/ppermute | solution.py:27
  401.2 7.7 %pad_maximum_fusion.1 = (f32[2,256,1536]{1,2,0:T(8,128)}, f32[2,512,1536]{1,2,0:T(8,128)}) fusion(f32[1,1024,1536]{1,2,0:T(8,128)} %bitcast.132, f32[1,1024,1536]{1,2,0:T(8,128)} %bitcast.129, f32[2,512,1536]{1,2,0:T(8,128)} %fusion.41, f32[2,256,1536]{1,2,0:T(8,128)} %collective-permute-done.2), kind=kLoop, calls=%fused_computation.62 | loop fusion | flops 2359296 | bytes 22020096 | tf_op jit(solution)/shard_map/stack | solution.py:114
  411.7 294.9 %all-reduce.3.cloned.1.call-done = f32[1536,1536]{0,1:T(8,128)} async-done(((f32[1536,1536]{0,1:T(8,128)}), f32[1536,1536]{0,1:T(8,128)}) %all-reduce.3.cloned.1.call-update) | async-done | bytes 9437200
  709.2 5.0 fusion.46
  (131 shorter events, 207.4 us)
Async XLA Ops:
  7.2 94.9 %copy-start = (bf16[512,1536]{1,0:T(8,128)(2,1)S(1)}, bf16[512,1536]{1,0:T(8,128)(2,1)}, u32[]{:S(2)}) copy-start(bf16[512,1536]{1,0:T(8,128)(2,1)} %param.15) | copy-start | bytes 4718596
  7.2 94.9 %all-gather.2.cloned.1.call-start = ((), (), s32[]{:S(2)}) async-start(), calls=%async_computation | async-start | bytes 5013504 | tf_op jit(solution)/shard_map/all_gather | solution.py:104
  7.9 698.7 %all-reduce.3.cloned.1.call-start = ((), (), s32[]{:S(2)}) async-start(), calls=%async_computation.1 | async-start | bytes 18874368
  15.5 71.7 %collective-permute-start = (bf16[2,256,1536]{1,2,0:T(8,128)(2,1)}, bf16[2,256,1536]{1,2,0:T(8,128)(2,1)}, u32[]{:S(2)}, u32[]{:S(2)}) collective-permute-start(bf16[2,256,1536]{1,2,0:T(8,128)(2,1)} %get-tuple-element.200), channel_id=1, source_target_pairs={{0,1},{1,2},{2,3},{3,4},{4,5},{5,6},{6,7},{7,8},{8,9},{9,10},{10,1... | collective-permute-start | bytes 4718600 | tf_op jit(solution)/shard_map/ppermute | solution.py:16
  20.8 66.4 %collective-permute-start.1 = (bf16[2,256,1536]{1,2,0:T(8,128)(2,1)}, bf16[2,256,1536]{1,2,0:T(8,128)(2,1)}, u32[]{:S(2)}, u32[]{:S(2)}) collective-permute-start(bf16[2,256,1536]{1,2,0:T(8,128)(2,1)} %get-tuple-element.201), channel_id=1, source_target_pairs={{1,0},{2,1},{3,2},{4,3},{5,4},{6,5},{7,6},{8,7},{9,8},{10,9},{11,1... | collective-permute-start | bytes 4718600 | tf_op jit(solution)/shard_map/ppermute | solution.py:19
  323.7 77.5 %collective-permute-start.2 = (f32[2,256,1536]{1,2,0:T(8,128)}, f32[2,256,1536]{1,2,0:T(8,128)}, u32[]{:S(2)}, u32[]{:S(2)}) collective-permute-start(f32[2,256,1536]{1,2,0:T(8,128)} %fusion.42), channel_id=1, source_target_pairs={{0,1},{1,2},{2,3},{3,4},{4,5},{5,6},{6,7},{7,8},{8,9},{9,10},{10,1... | collective-permute-start | bytes 9437192 | tf_op jit(solution)/shard_map/ppermute | solution.py:27
  339.4 70.8 %copy-start.1 = (bf16[12,512,128]{1,2,0:T(8,128)(2,1)S(1)}, bf16[12,512,128]{1,2,0:T(8,128)(2,1)}, u32[]{:S(2)}) copy-start(bf16[12,512,128]{1,2,0:T(8,128)(2,1)} %get-tuple-element.83) | copy-start | bytes 4718596
  408.9 300.3 %collective-permute-start.3 = (f32[2,256,1536]{1,2,0:T(8,128)}, f32[2,256,1536]{1,2,0:T(8,128)}, u32[]{:S(2)}, u32[]{:S(2)}) collective-permute-start(f32[2,256,1536]{1,2,0:T(8,128)} %get-tuple-element.194), channel_id=1, source_target_pairs={{1,0},{2,1},{3,2},{4,3},{5,4},{6,5},{7,6},{8,7},{9,8},{10,9},{11,1... | collective-permute-start | bytes 9437192 | tf_op jit(solution)/shard_map/ppermute | solution.py:27
Sparse Core Ops, SparseCore 0:
  9.8 92.1 all-gather.1
  333.2 373.4 all-reduce.2
where the time goes:
time: 732 us; the launch traced here: 730 us
  waiting for transfers between devices  427 us (58%)
  matrix products  183 us (25%)
  other arithmetic  71.6 us (10%)
  local copies, waits for them, and re-layouts  21.8 us (3%)
  between operations  14.8 us (2%)
  starting transfers between devices  10.8 us (1%)
    unnamed x3, waiting for transfers between devices  296 us
    ppermute x2, waiting for transfers between devices, passed_along(): return lax.ppermute(value, axis, pairs)  61.8 us
    ppermute x1, waiting for transfers between devices, extended(): lax.ppermute(lax.slice_in_dim(block, block.shape[dim] - width, None, axis...  61.8 us
    dot_general x12, matrix products, one_head(): jnp.dot(probability_b, value_head, preferred_element_type=jnp.float32)  40 us
    dot_general x12, matrix products, one_head(): lax.dot_general(grad_head, value_head, (((1,), (1,)), ((), ())), preferre...  29.5 us
    dot_general x12, matrix products, one_head(): lax.dot_general(probability_b, grad_head, (((0,), (0,)), ((), ())), prefe...  26.7 us
    dot_general x12, matrix products, one_head(): jnp.dot(grad_scores, key_head, preferred_element_type=jnp.float32)  25.2 us
    dot_general x12, matrix products, one_head(): lax.dot_general(query_head, key_head, (((1,), (1,)), ((), ())), preferred...  24.9 us
  transfers between devices with their start and end apart: 6, of which 4 were waited for; matrix products, arithmetic and copies ran while one was open for 6% of the time, Pallas kernels for 0%

commit v1 on v0

v1 whole, which is shorter than its diff:
```python
import jax
import jax.numpy as jnp
from jax import lax
from jax.experimental import pallas as pl
from jax.experimental.pallas import tpu as pltpu
from jax.sharding import PartitionSpec as P

HEAD_DIM = 128
HALF = 256
LOG2E = 1.4426950408889634


def dot_nt(a, b):
    return lax.dot_general(a, b, (((1,), (1,)), ((), ())), preferred_element_type=jnp.float32)


def dot_nn(a, b):
    return lax.dot_general(a, b, (((1,), (0,)), ((), ())), preferred_element_type=jnp.float32)


def dot_tn(a, b):
    return lax.dot_general(a, b, (((0,), (0,)), ((), ())), preferred_element_type=jnp.float32)


def attention_kernel(
    meta, q, k, v, gm, kl, vl, kr, vr, att, dq, dk, dv, dkl, dvl, dkr, dvr, bias
):
    rows = q.shape[0]
    width = 3 * HALF
    scale = HEAD_DIM ** (-0.5)
    first_row = meta[0]
    length = meta[1]

    @pl.when(pl.program_id(0) == 0)
    def _():
        for b in range(rows // HALF):
            start = first_row + b * HALF
            r = lax.broadcasted_iota(jnp.int32, (HALF, width), 0)
            c = lax.broadcasted_iota(jnp.int32, (HALF, width), 1)
            u = c + (start - HALF)
            ok = (c >= r) & (c < r + 2 * HALF) & (u >= 0) & (u < length)
            bias[b] = jnp.where(ok, 0.0, -1e30)

    k_all = [kl[...], k[0:HALF], k[HALF : 2 * HALF], kr[...]]
    v_all = [vl[...], v[0:HALF], v[HALF : 2 * HALF], vr[...]]
    dks, dvs = [], []
    for b in range(rows // HALF):
        lo, hi = b * HALF, (b + 1) * HALF
        qb, gb = q[lo:hi], gm[lo:hi]
        kc = jnp.concatenate(k_all[b : b + 3], axis=0)
        vc = jnp.concatenate(v_all[b : b + 3], axis=0)
        s = dot_nt(qb, kc) + bias[b]
        dp = dot_nt(gb, vc)
        m = jnp.max(s, axis=1, keepdims=True)
        e = jnp.exp2((s - m) * (scale * LOG2E))
        pos = first_row + lo + lax.broadcasted_iota(jnp.int32, (HALF, 1), 0)
        total = jnp.maximum(jnp.sum(e, axis=1, keepdims=True), 1.0)
        inv = jnp.where(pos < length, 1.0 / total, 0.0)
        p = e * inv
        pb = p.astype(jnp.bfloat16)
        att[lo:hi] = dot_nn(pb, vc).astype(att.dtype)
        delta = jnp.sum(p * dp, axis=1, keepdims=True)
        ds = (p * (dp - delta) * scale).astype(jnp.bfloat16)
        dq[lo:hi] = dot_nn(ds, kc).astype(dq.dtype)
        dks.append(dot_tn(ds, qb))
        dvs.append(dot_tn(pb, gb))
    for parts, left, own, right in ((dks, dkl, dk, dkr), (dvs, dvl, dv, dvr)):
        a, b = parts
        left[...] = a[0:HALF].astype(left.dtype)
        own[0:HALF] = (a[HALF : 2 * HALF] + b[0:HALF]).astype(own.dtype)
        own[HALF : 2 * HALF] = (a[2 * HALF :] + b[HALF : 2 * HALF]).astype(own.dtype)
        right[...] = b[2 * HALF :].astype(right.dtype)


def attention(meta, q, k, v, gm, kl, vl, kr, vr, heads=12, off=0):
    rows = q.shape[0]
    f32, bf16 = jnp.float32, jnp.bfloat16

    def whole(n, o=0):
        return pl.BlockSpec((n, HEAD_DIM), lambda h, s: (0, h + o))

    sds = jax.ShapeDtypeStruct
    w = heads * HEAD_DIM
    return pl.pallas_call(
        attention_kernel,
        name="attention",
        out_shape=[
            sds((rows, w), bf16),
            sds((rows, w), bf16),
            sds((rows, w), f32),
            sds((rows, w), f32),
            sds((HALF, w), bf16),
            sds((HALF, w), bf16),
            sds((HALF, w), bf16),
            sds((HALF, w), bf16),
        ],
        grid_spec=pltpu.PrefetchScalarGridSpec(
            num_scalar_prefetch=1,
            grid=(heads,),
            in_specs=[whole(rows, off)] * 3 + [whole(rows)] + [whole(HALF)] * 4,
            out_specs=[whole(rows)] * 4 + [whole(HALF)] * 4,
            scratch_shapes=[pltpu.VMEM((rows // HALF, HALF, 3 * HALF), f32)],
        ),
        compiler_params=pltpu.CompilerParams(dimension_semantics=("arbitrary",)),
    )(meta, q, k, v, gm, kl, vl, kr, vr)


def passed(value, axis, by):
    devices = lax.axis_size(axis)
    pairs = [(i, i + by) for i in range(devices) if 0 <= i + by < devices]
    return lax.ppermute(value, axis, pairs)


def halved(value, axis, bit, dim):
    mine = (lax.axis_index(axis) // bit) % 2 == 1
    low = lax.slice_in_dim(value, 0, 1, axis=dim)
    high = lax.slice_in_dim(value, 1, 2, axis=dim)
    pairs = [(i, i ^ bit) for i in range(lax.axis_size(axis))]
    sent = jnp.where(mine, low, high).astype(jnp.bfloat16)
    return jnp.where(mine, high, low) + lax.ppermute(sent, axis, pairs).astype(jnp.float32)


def scattered(part):
    cols = part.shape[1]
    part = part.reshape(2, 2, 2, 2, -1, cols)
    for bit, dim in ((1, 3), (4, 1), (8, 0)):
        part = halved(part, "dp", bit, dim)
    part = part.reshape(2, 2, 2, 2, 2, -1, cols)
    for axis, bit, dim in (("seq", 2, 3), ("seq", 4, 2), ("seq", 8, 1), ("dp", 2, 0), ("seq", 1, 4)):
        part = halved(part, axis, bit, dim)
    return part.reshape(-1, cols)


def shards(queries, keys, values, grad_out, out_weight, lengths):
    rows, width = queries.shape
    f32, bf16 = jnp.float32, jnp.bfloat16
    first_row = lax.axis_index("seq") * rows
    meta = jnp.stack([first_row, lengths[0]]).astype(jnp.int32)
    kl = passed(keys[rows - HALF :], "seq", 1)
    vl = passed(values[rows - HALF :], "seq", 1)
    kr = passed(keys[:HALF], "seq", -1)
    vr = passed(values[:HALF], "seq", -1)
    weight = lax.all_gather(out_weight, "dp", axis=0, tiled=True)
    grad_mixed = jnp.dot(grad_out, weight, preferred_element_type=f32).astype(bf16)
    att, dq, dk, dv, dkl, dvl, dkr, dvr = attention(
        meta, queries, keys, values, grad_mixed, kl, vl, kr, vr, heads=width // HEAD_DIM
    )
    outs = []
    for own, left, right in ((dk, dkl, dkr), (dv, dvl, dvr)):
        low = passed(right, "seq", 1).astype(f32)
        high = passed(left, "seq", -1).astype(f32)
        outs.append((own + jnp.concatenate([low, high], axis=0)).astype(bf16))
    part = lax.dot_general(
        grad_out, att, (((0,), (0,)), ((), ())), preferred_element_type=f32
    )
    return dq, outs[0], outs[1], scattered(part)


def solution(mesh):
    rows = P(("dp", "seq"), None)
    return jax.shard_map(
        shards,
        mesh=mesh,
        in_specs=(rows, rows, rows, rows, P("dp", None), P("dp")),
        out_specs=(rows, rows, rows, rows),
        check_vma=False,
    )
```

time: 732 us -> 342 us (0.47)
  waiting for transfers between devices: 427 us -> 183 us
  matrix products: 183 us -> 12.5 us
  starting transfers between devices: 10.8 us -> 51.1 us
  other arithmetic: 71.6 us -> 39.5 us
  Pallas kernels: 0 us -> 27.1 us
  local copies, waits for them, and re-layouts: 21.8 us -> 12.9 us
    unnamed x3 -> x1, waiting for transfers between devices: 296 us -> 0.68 us
    dot_general x74 -> x2, matrix products: 183 us -> 12.5 us  [the longest x1 6.53 us: shards(): lax.dot_general(grad_out, att, (((0,), (0,)), ((), ())), preferred_elemen...]
    all_gather x1, waiting for transfers between devices: 8.01 us -> 65.6 us  [shards(): weight = lax.all_gather(out_weight, 'dp', axis=0, tiled=True)]
    ppermute x4 -> x16, starting transfers between devices: 10.7 us -> 51.1 us  [the longest x8 28.7 us: passed(): return lax.ppermute(value, axis, pairs)]
    pallas_call x0 -> x1, Pallas kernels: none -> 27.1 us  [attention(): pl.pallas_call(attention_kernel, name='attention', out_shape=[sds((rows,...]
    another operation x9 -> x1, other arithmetic: 24.1 us -> 0.59 us  [shards(): meta = jnp.stack([first_row, lengths[0]]).astype(jnp.int32)]
    add x2 -> x8, other arithmetic: 0.01 us -> 21.3 us  [halved(): jnp.where(mine, high, low)]
    reduce_sum x12 -> x0, other arithmetic: 18.8 us -> none  [one_head(): row_total = jnp.maximum(jnp.sum(expo, axis=1, keepdims=True), 1.0)]
  transfers between devices with their start and end apart: 6 -> 17, of which waited for: 4 -> 9; matrix products, arithmetic and copies ran while one was open for 6% -> 5% of each run, Pallas kernels for 0% -> 0%
where the time goes in v1:
time: 342 us; the launch traced here: 341 us
  waiting for transfers between devices  183 us (54%)
  starting transfers between devices  51.1 us (15%)
  other arithmetic  39.5 us (12%)
  Pallas kernels  27.1 us (8%)
  between operations  15 us (4%)
  local copies, waits for them, and re-layouts  12.9 us (4%)
  matrix products  12.5 us (4%)
    ppermute x8, waiting for transfers between devices, halved(): lax.ppermute(sent, axis, pairs).astype(jnp.float32)  77.5 us
    all_gather x1, waiting for transfers between devices, shards(): weight = lax.all_gather(out_weight, 'dp', axis=0, tiled=True)  65.6 us
    ppermute x8, waiting for transfers between devices, passed(): return lax.ppermute(value, axis, pairs)  39.6 us
    ppermute x8, starting transfers between devices, passed(): return lax.ppermute(value, axis, pairs)  28.7 us
    pallas_call x1, Pallas kernels, attention(): pl.pallas_call(attention_kernel, name='attention', out_shape=[sds((rows,...  27.1 us
    ppermute x8, starting transfers between devices, halved(): lax.ppermute(sent, axis, pairs).astype(jnp.float32)  22.4 us
    add x8, other arithmetic, halved(): jnp.where(mine, high, low)  21.3 us
    convert_element_type x8, other arithmetic, halved(): sent = jnp.where(mine, low, high).astype(jnp.bfloat16)  12.4 us
  transfers between devices with their start and end apart: 17, of which 9 were waited for; matrix products, arithmetic and copies ran while one was open for 5% of the time, Pallas kernels for 0%

profile of v1, /device:TPU:18, one launch (start us, length us, event | category | flops | bytes accessed | tf_op | source)
XLA Modules:
  0.0 341.4 jit_solution(2502522252339655398)
XLA Ops:
  11.8 7.0 %collective-permute-start = (bf16[256,1536]{1,0:T(8,128)(2,1)}, bf16[256,1536]{1,0:T(8,128)(2,1)}, u32[]{:S(2)}, u32[]{:S(2)}) collective-permute-start(bf16[256,1536]{1,0:T(8,128)(2,1)} %get-tuple-element.25), channel_id=1, source_target_pairs={{0,1},{1,2},{2,3},{3,4},{4,5},{5,6},{6,7},{7,8},{8,9},{9,10},{10,1... | collective-permute-start | bytes 2359304 | tf_op jit(solution)/shard_map/ppermute | solution.py:111
  21.4 6.1 %collective-permute-start.1 = (bf16[256,1536]{1,0:T(8,128)(2,1)}, bf16[256,1536]{1,0:T(8,128)(2,1)S(1)}, u32[]{:S(2)}, u32[]{:S(2)}) collective-permute-start(bf16[256,1536]{1,0:T(8,128)(2,1)} %get-tuple-element.23), channel_id=1, source_target_pairs={{0,1},{1,2},{2,3},{3,4},{4,5},{5,6},{6,7},{7,8},{8,9},{9,10},{10,1... | collective-permute-start | bytes 2359304 | tf_op jit(solution)/shard_map/ppermute | solution.py:111
  28.7 65.6 %all-gather.2.cloned.1.call-done = bf16[1536,1536]{1,0:T(8,128)(2,1)} async-done(((bf16[96,1536]{1,0:T(8,128)(2,1)}), bf16[1536,1536]{1,0:T(8,128)(2,1)}) %all-gather.2.cloned.1.call-update) | async-done | bytes 4718608 | tf_op jit(solution)/shard_map/all_gather | solution.py:143
  94.3 6.0 %convolution_convert_fusion.gm = bf16[512,1536]{1,0:T(8,128)(2,1)} fusion(bf16[512,1536]{1,0:T(8,128)(2,1)S(1)} %copy-done, bf16[1536,1536]{1,0:T(8,128)(2,1)} %all-gather.2.cloned.1.call-done), kind=kOutput, calls=%fused_computation.4 | convolution fusion | flops 2416705536 | bytes 7864320 | tf_op jit(solution)/shard_map/dot_general | solution.py:144
  102.1 27.1 %attention.1 = (bf16[512,1536]{1,0:T(8,128)(2,1)}, bf16[512,1536]{1,0:T(8,128)(2,1)}, f32[512,1536]{1,0:T(8,128)}, f32[512,1536]{1,0:T(8,128)}, bf16[256,1536]{1...) custom-call(s32[2]{0:T(128)} %pad_add_fusion.meta, ...), custom_call_target="tpu_custom_call" | custom-call | tf_op jit(solution)/shard_map/attention/pallas_call | solution.py:84
  129.2 6.5 %fusion.7 = f32[1536,1536]{0,1:T(8,128)} fusion(bf16[512,1536]{1,0:T(8,128)(2,1)} %get-tuple-element.19, bf16[512,1536]{1,0:T(8,128)(2,1)S(1)} %copy-done), kind=kOutput, calls=%fused_computation.28 | convolution fusion | flops 2415919104 | bytes 12582912 | tf_op jit(solution)/shard_map/dot_general | solution.py:153
  135.7 5.1 %fusion.4 = (f32[2,2,2,1,96,1536]{5,4,3,2,1,0:T(8,128)S(1)}, f32[2,2,2,1,96,1536]{5,4,3,2,1,0:T(8,128)S(1)}) fusion(f32[2,2,2,2,96,1536]{5,4,3,2,1,0:T(8,128)} %bitcast.12), kind=kLoop, calls=%fused_computation.25 | loop fusion | bytes 18874368 | tf_op jit(solution)/shard_map/slice | solution.py:117
  140.9 7.5 %select_convert_fusion = bf16[2,2,2,1,96,1536]{5,2,4,3,1,0:T(2,128)(2,1)} fusion(pred[]{:T(512)S(6)} %eq.40, f32[2,2,2,1,96,1536]{5,4,3,2,1,0:T(8,128)S(1)} %get-tuple-element.21, f32[2,2,2,1,96,1536]{5,4,3,2,1,0:T(8,128)S(1)} %get-tuple-element.20), kind=kLoop, calls=%fused_computation.1 | loop fusion | flops 1179648 | bytes 11796481 | tf_op jit(solution)/shard_map/convert_element_type | solution.py:119
  148.5 4.7 %collective-permute-done.8 = bf16[2,2,2,1,96,1536]{5,2,4,3,1,0:T(2,128)(2,1)} collective-permute-done((bf16[2,2,2,1,96,1536]{5,2,4,3,1,0:T(2,128)(2,1)}, bf16[2,2,2,1,96,1536]{5,2,4,3,1,0:T(2,128)(2,1)}, u32[]{:S(2)}, u32[]{:S(2)}) %collective-permute-start.8) | collective-permute-done | bytes 2359328 | tf_op jit(solution)/shard_map/ppermute | solution.py:120
  153.2 13.9 %convert_add_fusion = f32[2,2,2,1,96,1536]{5,2,4,3,1,0:T(2,128)} fusion(bf16[2,2,2,1,96,1536]{5,2,4,3,1,0:T(2,128)(2,1)} %collective-permute-done.8, pred[]{:T(512)S(6)} %eq.40, f32[2,2,2,1,96,1536]{5,4,3,2,1,0:T(8,128)} %copy-done.3, f32[2,2,2,1,96,1536]{5,4,3,2,1,0:T(8,128)} %copy-done.2), kind=kLoop, calls=%fused_computation | loop fusion | flops 3538944 | bytes 16515073 | tf_op jit(solution)/shard_map/add | solution.py:120
  170.7 5.6 %collective-permute-start.9 = (bf16[2,1,2,1,96,1536]{5,2,4,3,1,0:T(2,128)(2,1)S(1)}, bf16[2,1,2,1,96,1536]{5,2,4,3,1,0:T(2,128)(2,1)S(1)}, u32[]{:S(2)}, u32[]{:S(2)}) collective-permute-start(bf16[2,1,2,1,96,1536]{5,2,4,3,1,0:T(2,128)(2,1)S(1)} %select_convert_fusion.1), channel_id=1, source_target_pairs={{0,64},{16,80},{32,96},{48,112},{64,0},{80,16},{96,32},{112,48},{1... | collective-permute-start | bytes 3538952 | tf_op jit(solution)/shard_map/ppermute | solution.py:120
  176.4 26.3 %collective-permute-done.9 = bf16[2,1,2,1,96,1536]{5,2,4,3,1,0:T(2,128)(2,1)S(1)} collective-permute-done((bf16[2,1,2,1,96,1536]{5,2,4,3,1,0:T(2,128)(2,1)S(1)}, bf16[2,1,2,1,96,1536]{5,2,4,3,1,0:T(2,128)(2,1)S(1)}, u32[]{:S(2)}, u32[]{:S(2)}) %collective-permute-start.9) | collective-permute-done | bytes 1179680 | tf_op jit(solution)/shard_map/ppermute | solution.py:120
  202.6 4.0 %convert_add_fusion.1 = f32[2,1,2,1,96,1536]{5,2,4,3,1,0:T(2,128)S(1)} fusion(bf16[2,1,2,1,96,1536]{5,2,4,3,1,0:T(2,128)(2,1)S(1)} %collective-permute-done.9, pred[]{:T(512)S(6)} %eq.39, f32[2,2,2,1,96,1536]{5,2,4,3,1,0:T(2,128)} %convert_add_fusion), kind=kLoop, calls=%fused_computation.5 | loop fusion | flops 1769472 | bytes 8257537 | tf_op jit(solution)/shard_map/add | solution.py:120
  209.6 15.5 %collective-permute-done.10 = bf16[1,1,2,1,96,1536]{5,2,4,3,1,0:T(2,128)(2,1)S(1)} collective-permute-done((bf16[1,1,2,1,96,1536]{5,2,4,3,1,0:T(2,128)(2,1)S(1)}, bf16[1,1,2,1,96,1536]{5,2,4,3,1,0:T(2,128)(2,1)S(1)}, u32[]{:S(2)}, u32[]{:S(2)}) %collective-permute-start.10) | collective-permute-done | bytes 589856 | tf_op jit(solution)/shard_map/ppermute | solution.py:120
  227.8 3.8 %collective-permute-start.11 = (bf16[2,2,2,1,2,6,1536]{6,0,5,4,3,2,1:T(2,128)(2,1)S(1)}, bf16[2,2,2,1,2,6,1536]{6,0,5,4,3,2,1:T(2,128)(2,1)S(1)}, u32[]{:S(2)}, u32[]{:S(2)}) collective-permute-start(bf16[2,2,2,1,2,6,1536]{6,0,5,4,3,2,1:T(2,128)(2,1)S(1)} %select_convert_fusion.3), channel_id=1, source_target_pairs={{0,2},{1,3},{2,0},{3,1},{4,6},{5,7},{6,4},{7,5},{8,10},{9,11},{10,... | collective-permute-start | bytes 884744 | tf_op jit(solution)/shard_map/ppermute | solution.py:120
  231.6 5.9 %collective-permute-done.11 = bf16[2,2,2,1,2,6,1536]{6,0,5,4,3,2,1:T(2,128)(2,1)S(1)} collective-permute-done((bf16[2,2,2,1,2,6,1536]{6,0,5,4,3,2,1:T(2,128)(2,1)S(1)}, bf16[2,2,2,1,2,6,1536]{6,0,5,4,3,2,1:T(2,128)(2,1)S(1)}, u32[]{:S(2)}, u32[]{:S(2)}) %collective-permute-start.11) | collective-permute-done | bytes 294944 | tf_op jit(solution)/shard_map/ppermute | solution.py:120
  241.4 5.2 %collective-permute-done.12 = bf16[2,2,1,1,2,6,1536]{6,0,5,4,3,2,1:T(2,128)(2,1)S(1)} collective-permute-done((bf16[2,2,1,1,2,6,1536]{6,0,5,4,3,2,1:T(2,128)(2,1)S(1)}, bf16[2,2,1,1,2,6,1536]{6,0,5,4,3,2,1:T(2,128)(2,1)S(1)}, u32[]{:S(2)}, u32[]{:S(2)}) %collective-permute-start.12) | collective-permute-done | bytes 147488 | tf_op jit(solution)/shard_map/ppermute | solution.py:120
  246.9 6.4 %collective-permute-start.13 = (bf16[2,1,1,1,2,6,1536]{6,0,5,4,3,2,1:T(2,128)(2,1)S(1)}, bf16[2,1,1,1,2,6,1536]{6,0,5,4,3,2,1:T(2,128)(2,1)S(1)}, u32[]{:S(2)}, u32[]{:S(2)}) collective-permute-start(bf16[2,1,1,1,2,6,1536]{6,0,5,4,3,2,1:T(2,128)(2,1)S(1)} %select_convert_fusion.5), channel_id=1, source_target_pairs={{0,8},{1,9},{2,10},{3,11},{4,12},{5,13},{6,14},{7,15},{8,0},{9,1},... | collective-permute-start | bytes 221192 | tf_op jit(solution)/shard_map/ppermute | solution.py:120
  253.3 4.4 %collective-permute-start.4 = (bf16[256,1536]{1,0:T(8,128)(2,1)}, bf16[256,1536]{1,0:T(8,128)(2,1)S(1)}, u32[]{:S(2)}, u32[]{:S(2)}) collective-permute-start(bf16[256,1536]{1,0:T(8,128)(2,1)} %get-tuple-element.14), channel_id=1, source_target_pairs={{0,1},{1,2},{2,3},{3,4},{4,5},{5,6},{6,7},{7,8},{8,9},{9,10},{10,1... | collective-permute-start | bytes 2359304 | tf_op jit(solution)/shard_map/ppermute | solution.py:111
  259.0 6.1 %collective-permute-start.6 = (bf16[256,1536]{1,0:T(8,128)(2,1)}, bf16[256,1536]{1,0:T(8,128)(2,1)S(1)}, u32[]{:S(2)}, u32[]{:S(2)}) collective-permute-start(bf16[256,1536]{1,0:T(8,128)(2,1)} %get-tuple-element.17), channel_id=1, source_target_pairs={{0,1},{1,2},{2,3},{3,4},{4,5},{5,6},{6,7},{7,8},{8,9},{9,10},{10,1... | collective-permute-start | bytes 2359304 | tf_op jit(solution)/shard_map/ppermute | solution.py:111
  268.7 39.6 %collective-permute-done.4 = bf16[256,1536]{1,0:T(8,128)(2,1)S(1)} collective-permute-done((bf16[256,1536]{1,0:T(8,128)(2,1)}, bf16[256,1536]{1,0:T(8,128)(2,1)S(1)}, u32[]{:S(2)}, u32[]{:S(2)}) %collective-permute-start.4) | collective-permute-done | bytes 786464 | tf_op jit(solution)/shard_map/ppermute | solution.py:111
  308.3 3.6 %add_convert_fusion.1 = bf16[512,1536]{1,0:T(8,128)(2,1)} fusion(f32[512,1536]{1,0:T(8,128)} %get-tuple-element.13, bf16[256,1536]{1,0:T(8,128)(2,1)S(1)} %collective-permute-done.5, bf16[256,1536]{1,0:T(8,128)(2,1)S(1)} %collective-permute-done.4), kind=kLoop, calls=%fused_computation.3 | loop fusion | flops 4718592 | bytes 6291456 | tf_op jit(solution)/shard_map/convert_element_type | solution.py:152
  311.9 16.2 %collective-permute-done.14 = bf16[1,1,1,1,2,6,1536]{6,0,5,4,3,2,1:T(2,128)(2,1)S(1)} collective-permute-done((bf16[1,1,1,1,2,6,1536]{6,0,5,4,3,2,1:T(2,128)(2,1)S(1)}, bf16[1,1,1,1,2,6,1536]{6,0,5,4,3,2,1:T(2,128)(2,1)S(1)}, u32[]{:S(2)}, u32[]{:S(2)}) %collective-permute-start.14) | collective-permute-done | bytes 36896 | tf_op jit(solution)/shard_map/ppermute | solution.py:120
  330.1 3.8 %collective-permute-done.15 = bf16[1,1,1,1,1,6,1536]{6,0,5,4,3,2,1:T(2,128)(2,1)S(1)} collective-permute-done((bf16[1,1,1,1,1,6,1536]{6,0,5,4,3,2,1:T(2,128)(2,1)S(1)}, bf16[1,1,1,1,1,6,1536]{6,0,5,4,3,2,1:T(2,128)(2,1)S(1)}, u32[]{:S(2)}, u32[]{:S(2)}) %collective-permute-start.15) | collective-permute-done | bytes 18464 | tf_op jit(solution)/shard_map/ppermute | solution.py:120
  (57 shorter events, 30.7 us)
Async XLA Ops:
  7.2 87.1 %copy-start = (bf16[512,1536]{1,0:T(8,128)(2,1)S(1)}, bf16[512,1536]{1,0:T(8,128)(2,1)}, u32[]{:S(2)}) copy-start(bf16[512,1536]{1,0:T(8,128)(2,1)} %param.9) | copy-start | bytes 4718596
  7.2 11.6 %copy-start.5 = (bf16[512,1536]{1,0:T(8,128)(2,1)S(1)}, bf16[512,1536]{1,0:T(8,128)(2,1)}, u32[]{:S(2)}) copy-start(bf16[512,1536]{1,0:T(8,128)(2,1)} %v.1) | copy-start | bytes 4718596
  7.2 87.1 %all-gather.2.cloned.1.call-start = ((), (), s32[]{:S(2)}) async-start(), calls=%async_computation | async-start | bytes 5013504 | tf_op jit(solution)/shard_map/all_gather | solution.py:143
  10.5 89.7 %collective-permute-start.2 = (bf16[256,1536]{1,0:T(8,128)(2,1)}, bf16[256,1536]{1,0:T(8,128)(2,1)}, u32[]{:S(2)}, u32[]{:S(2)}) collective-permute-start(bf16[256,1536]{1,0:T(8,128)(2,1)} %get-tuple-element.24), channel_id=1, source_target_pairs={{1,0},{2,1},{3,2},{4,3},{5,4},{6,5},{7,6},{8,7},{9,8},{10,9},{11,1... | collective-permute-start | bytes 2359304 | tf_op jit(solution)/shard_map/ppermute | solution.py:111
  11.8 88.5 %collective-permute-start = (bf16[256,1536]{1,0:T(8,128)(2,1)}, bf16[256,1536]{1,0:T(8,128)(2,1)}, u32[]{:S(2)}, u32[]{:S(2)}) collective-permute-start(bf16[256,1536]{1,0:T(8,128)(2,1)} %get-tuple-element.25), channel_id=1, source_target_pairs={{0,1},{1,2},{2,3},{3,4},{4,5},{5,6},{6,7},{7,8},{8,9},{9,10},{10,1... | collective-permute-start | bytes 2359304 | tf_op jit(solution)/shard_map/ppermute | solution.py:111
  20.1 80.2 %collective-permute-start.3 = (bf16[256,1536]{1,0:T(8,128)(2,1)}, bf16[256,1536]{1,0:T(8,128)(2,1)S(1)}, u32[]{:S(2)}, u32[]{:S(2)}) collective-permute-start(bf16[256,1536]{1,0:T(8,128)(2,1)} %get-tuple-element.22), channel_id=1, source_target_pairs={{1,0},{2,1},{3,2},{4,3},{5,4},{6,5},{7,6},{8,7},{9,8},{10,9},{11,1... | collective-permute-start | bytes 2359304 | tf_op jit(solution)/shard_map/ppermute | solution.py:111
  21.4 79.0 %collective-permute-start.1 = (bf16[256,1536]{1,0:T(8,128)(2,1)}, bf16[256,1536]{1,0:T(8,128)(2,1)S(1)}, u32[]{:S(2)}, u32[]{:S(2)}) collective-permute-start(bf16[256,1536]{1,0:T(8,128)(2,1)} %get-tuple-element.23), channel_id=1, source_target_pairs={{0,1},{1,2},{2,3},{3,4},{4,5},{5,6},{6,7},{7,8},{8,9},{9,10},{10,1... | collective-permute-start | bytes 2359304 | tf_op jit(solution)/shard_map/ppermute | solution.py:111
  140.8 7.5 %copy-start.2 = (f32[2,2,2,1,96,1536]{5,4,3,2,1,0:T(8,128)}, f32[2,2,2,1,96,1536]{5,4,3,2,1,0:T(8,128)S(1)}, u32[]{:S(2)}) copy-start(f32[2,2,2,1,96,1536]{5,4,3,2,1,0:T(8,128)S(1)} %get-tuple-element.20) | copy-start | bytes 14155780
  140.8 7.5 %copy-start.3 = (f32[2,2,2,1,96,1536]{5,4,3,2,1,0:T(8,128)}, f32[2,2,2,1,96,1536]{5,4,3,2,1,0:T(8,128)S(1)}, u32[]{:S(2)}) copy-start(f32[2,2,2,1,96,1536]{5,4,3,2,1,0:T(8,128)S(1)} %get-tuple-element.21) | copy-start | bytes 14155780
  148.3 4.9 %collective-permute-start.8 = (bf16[2,2,2,1,96,1536]{5,2,4,3,1,0:T(2,128)(2,1)}, bf16[2,2,2,1,96,1536]{5,2,4,3,1,0:T(2,128)(2,1)}, u32[]{:S(2)}, u32[]{:S(2)}) collective-permute-start(bf16[2,2,2,1,96,1536]{5,2,4,3,1,0:T(2,128)(2,1)} %select_convert_fusion), channel_id=1, source_target_pairs={{0,16},{16,0},{32,48},{48,32},{64,80},{80,64},{96,112},{112,96},{1... | collective-permute-start | bytes 7077896 | tf_op jit(solution)/shard_map/ppermute | solution.py:120
  170.7 31.9 %collective-permute-start.9 = (bf16[2,1,2,1,96,1536]{5,2,4,3,1,0:T(2,128)(2,1)S(1)}, bf16[2,1,2,1,96,1536]{5,2,4,3,1,0:T(2,128)(2,1)S(1)}, u32[]{:S(2)}, u32[]{:S(2)}) collective-permute-start(bf16[2,1,2,1,96,1536]{5,2,4,3,1,0:T(2,128)(2,1)S(1)} %select_convert_fusion.1), channel_id=1, source_target_pairs={{0,64},{16,80},{32,96},{48,112},{64,0},{80,16},{96,32},{112,48},{1... | collective-permute-start | bytes 3538952 | tf_op jit(solution)/shard_map/ppermute | solution.py:120
  208.7 16.4 %collective-permute-start.10 = (bf16[1,1,2,1,96,1536]{5,2,4,3,1,0:T(2,128)(2,1)S(1)}, bf16[1,1,2,1,96,1536]{5,2,4,3,1,0:T(2,128)(2,1)S(1)}, u32[]{:S(2)}, u32[]{:S(2)}) collective-permute-start(bf16[1,1,2,1,96,1536]{5,2,4,3,1,0:T(2,128)(2,1)S(1)} %select_convert_fusion.2), channel_id=1, source_target_pairs={{0,128},{16,144},{32,160},{48,176},{64,192},{80,208},{96,224},{112... | collective-permute-start | bytes 1769480 | tf_op jit(solution)/shard_map/ppermute | solution.py:120
  227.5 37.6 %copy-start.9 = (bf16[256,1536]{1,0:T(8,128)(2,1)S(1)}, bf16[256,1536]{1,0:T(8,128)(2,1)}, u32[]{:S(2)}) copy-start(bf16[256,1536]{1,0:T(8,128)(2,1)} %get-tuple-element.18) | copy-start | bytes 2359300
  227.8 9.6 %collective-permute-start.11 = (bf16[2,2,2,1,2,6,1536]{6,0,5,4,3,2,1:T(2,128)(2,1)S(1)}, bf16[2,2,2,1,2,6,1536]{6,0,5,4,3,2,1:T(2,128)(2,1)S(1)}, u32[]{:S(2)}, u32[]{:S(2)}) collective-permute-start(bf16[2,2,2,1,2,6,1536]{6,0,5,4,3,2,1:T(2,128)(2,1)S(1)} %select_convert_fusion.3), channel_id=1, source_target_pairs={{0,2},{1,3},{2,0},{3,1},{4,6},{5,7},{6,4},{7,5},{8,10},{9,11},{10,... | collective-permute-start | bytes 884744 | tf_op jit(solution)/shard_map/ppermute | solution.py:120
  238.0 8.6 %collective-permute-start.12 = (bf16[2,2,1,1,2,6,1536]{6,0,5,4,3,2,1:T(2,128)(2,1)S(1)}, bf16[2,2,1,1,2,6,1536]{6,0,5,4,3,2,1:T(2,128)(2,1)S(1)}, u32[]{:S(2)}, u32[]{:S(2)}) collective-permute-start(bf16[2,2,1,1,2,6,1536]{6,0,5,4,3,2,1:T(2,128)(2,1)S(1)} %select_convert_fusion.4), channel_id=1, source_target_pairs={{0,4},{1,5},{2,6},{3,7},{4,0},{5,1},{6,2},{7,3},{8,12},{9,13},{10,... | collective-permute-start | bytes 442376 | tf_op jit(solution)/shard_map/ppermute | solution.py:120
  246.9 19.6 %collective-permute-start.13 = (bf16[2,1,1,1,2,6,1536]{6,0,5,4,3,2,1:T(2,128)(2,1)S(1)}, bf16[2,1,1,1,2,6,1536]{6,0,5,4,3,2,1:T(2,128)(2,1)S(1)}, u32[]{:S(2)}, u32[]{:S(2)}) collective-permute-start(bf16[2,1,1,1,2,6,1536]{6,0,5,4,3,2,1:T(2,128)(2,1)S(1)} %select_convert_fusion.5), channel_id=1, source_target_pairs={{0,8},{1,9},{2,10},{3,11},{4,12},{5,13},{6,14},{7,15},{8,0},{9,1},... | collective-permute-start | bytes 221192 | tf_op jit(solution)/shard_map/ppermute | solution.py:120
  253.3 55.0 %collective-permute-start.4 = (bf16[256,1536]{1,0:T(8,128)(2,1)}, bf16[256,1536]{1,0:T(8,128)(2,1)S(1)}, u32[]{:S(2)}, u32[]{:S(2)}) collective-permute-start(bf16[256,1536]{1,0:T(8,128)(2,1)} %get-tuple-element.14), channel_id=1, source_target_pairs={{0,1},{1,2},{2,3},{3,4},{4,5},{5,6},{6,7},{7,8},{8,9},{9,10},{10,1... | collective-permute-start | bytes 2359304 | tf_op jit(solution)/shard_map/ppermute | solution.py:111
  257.7 50.6 %collective-permute-start.5 = (bf16[256,1536]{1,0:T(8,128)(2,1)}, bf16[256,1536]{1,0:T(8,128)(2,1)S(1)}, u32[]{:S(2)}, u32[]{:S(2)}) collective-permute-start(bf16[256,1536]{1,0:T(8,128)(2,1)} %get-tuple-element.15), channel_id=1, source_target_pairs={{1,0},{2,1},{3,2},{4,3},{5,4},{6,5},{7,6},{8,7},{9,8},{10,9},{11,1... | collective-permute-start | bytes 2359304 | tf_op jit(solution)/shard_map/ppermute | solution.py:111
  259.0 69.4 %collective-permute-start.6 = (bf16[256,1536]{1,0:T(8,128)(2,1)}, bf16[256,1536]{1,0:T(8,128)(2,1)S(1)}, u32[]{:S(2)}, u32[]{:S(2)}) collective-permute-start(bf16[256,1536]{1,0:T(8,128)(2,1)} %get-tuple-element.17), channel_id=1, source_target_pairs={{0,1},{1,2},{2,3},{3,4},{4,5},{5,6},{6,7},{7,8},{8,9},{9,10},{10,1... | collective-permute-start | bytes 2359304 | tf_op jit(solution)/shard_map/ppermute | solution.py:111
  265.1 63.3 %collective-permute-start.7 = (bf16[256,1536]{1,0:T(8,128)(2,1)S(1)}, bf16[256,1536]{1,0:T(8,128)(2,1)S(1)}, u32[]{:S(2)}, u32[]{:S(2)}) collective-permute-start(bf16[256,1536]{1,0:T(8,128)(2,1)S(1)} %copy-done.9), channel_id=1, source_target_pairs={{1,0},{2,1},{3,2},{4,3},{5,4},{6,5},{7,6},{8,7},{9,8},{10,9},{11,1... | collective-permute-start | bytes 2359304 | tf_op jit(solution)/shard_map/ppermute | solution.py:111
  266.7 61.5 %collective-permute-start.14 = (bf16[1,1,1,1,2,6,1536]{6,0,5,4,3,2,1:T(2,128)(2,1)S(1)}, bf16[1,1,1,1,2,6,1536]{6,0,5,4,3,2,1:T(2,128)(2,1)S(1)}, u32[]{:S(2)}, u32[]{:S(2)}) collective-permute-start(bf16[1,1,1,1,2,6,1536]{6,0,5,4,3,2,1:T(2,128)(2,1)S(1)} %fusion.1), channel_id=1, source_target_pairs={{0,32},{16,48},{32,0},{48,16},{64,96},{80,112},{96,64},{112,80},{1... | collective-permute-start | bytes 110600 | tf_op jit(solution)/shard_map/ppermute | solution.py:120
  308.3 20.2 %copy-start.6 = (f32[512,1536]{1,0:T(8,128)S(1)}, f32[512,1536]{1,0:T(8,128)}, u32[]{:S(2)}) copy-start(f32[512,1536]{1,0:T(8,128)} %get-tuple-element.16) | copy-start | bytes 9437188
  328.3 5.5 %collective-permute-start.15 = (bf16[1,1,1,1,1,6,1536]{6,0,5,4,3,2,1:T(2,128)(2,1)S(1)}, bf16[1,1,1,1,1,6,1536]{6,0,5,4,3,2,1:T(2,128)(2,1)S(1)}, u32[]{:S(2)}, u32[]{:S(2)}) collective-permute-start(bf16[1,1,1,1,1,6,1536]{6,0,5,4,3,2,1:T(2,128)(2,1)S(1)} %fusion.3), channel_id=1, source_target_pairs={{0,1},{1,0},{2,3},{3,2},{4,5},{5,4},{6,7},{7,6},{8,9},{9,8},{10,11... | collective-permute-start | bytes 55304 | tf_op jit(solution)/shard_map/ppermute | solution.py:120
  328.5 6.1 %copy-start.1 = (bf16[512,1536]{1,0:T(8,128)(2,1)S(1)}, bf16[512,1536]{1,0:T(8,128)(2,1)}, u32[]{:S(2)}) copy-start(bf16[512,1536]{1,0:T(8,128)(2,1)} %param.9) | copy-start | bytes 4718596
  (3 other events, 3.2 us)
Sparse Core Ops, SparseCore 0:
  9.8 84.3 all-gather.1

commit v2 on v1

v2 whole, which is shorter than its diff:
```python
import jax
import jax.numpy as jnp
from jax import lax
from jax.experimental import pallas as pl
from jax.experimental.pallas import tpu as pltpu
from jax.sharding import PartitionSpec as P


HEAD_DIM = 128
HALF = 256
LOG2E = 1.4426950408889634
F32 = jnp.float32
BF16 = jnp.bfloat16
ANY = pl.BlockSpec(memory_space=pl.ANY)
SDS = jax.ShapeDtypeStruct


def dot_nt(a, b):
    return lax.dot_general(a, b, (((1,), (1,)), ((), ())), preferred_element_type=F32)


def dot_nn(a, b):
    return lax.dot_general(a, b, (((1,), (0,)), ((), ())), preferred_element_type=F32)


def dot_tn(a, b):
    return lax.dot_general(a, b, (((0,), (0,)), ((), ())), preferred_element_type=F32)


def attention_kernel(meta, q, k, v, gm, left, right, *refs):
    att, dq, dk, dv, gl, gr, bias = refs[-7:]
    rows = q.shape[0]
    width = 3 * HALF
    scale = HEAD_DIM ** (-0.5)
    first_row = meta[0]
    length = meta[1]

    @pl.when(pl.program_id(0) == 0)
    def _():
        for b in range(rows // HALF):
            start = first_row + b * HALF
            r = lax.broadcasted_iota(jnp.int32, (HALF, width), 0)
            c = lax.broadcasted_iota(jnp.int32, (HALF, width), 1)
            u = c + (start - HALF)
            ok = (c >= r) & (c < r + 2 * HALF) & (u >= 0) & (u < length)
            bias[b] = jnp.where(ok, 0.0, -1e30)

    k_all = [left[0], k[0:HALF], k[HALF : 2 * HALF], right[0]]
    v_all = [left[1], v[0:HALF], v[HALF : 2 * HALF], right[1]]
    dks, dvs = [], []
    for b in range(rows // HALF):
        lo, hi = b * HALF, (b + 1) * HALF
        qb, gb = q[lo:hi], gm[lo:hi]
        kc = jnp.concatenate(k_all[b : b + 3], axis=0)
        vc = jnp.concatenate(v_all[b : b + 3], axis=0)
        s = dot_nt(qb, kc) + bias[b]
        dp = dot_nt(gb, vc)
        m = jnp.max(s, axis=1, keepdims=True)
        e = jnp.exp2((s - m) * (scale * LOG2E))
        pos = first_row + lo + lax.broadcasted_iota(jnp.int32, (HALF, 1), 0)
        total = jnp.maximum(jnp.sum(e, axis=1, keepdims=True), 1.0)
        inv = jnp.where(pos < length, 1.0 / total, 0.0)
        p = e * inv
        pb = p.astype(BF16)
        att[lo:hi] = dot_nn(pb, vc).astype(att.dtype)
        delta = jnp.sum(p * dp, axis=1, keepdims=True)
        ds = (p * (dp - delta) * scale).astype(BF16)
        dq[lo:hi] = dot_nn(ds, kc).astype(dq.dtype)
        dks.append(dot_tn(ds, qb))
        dvs.append(dot_tn(pb, gb))
    for n, (parts, own) in enumerate(((dks, dk), (dvs, dv))):
        a, b = parts
        gl[n] = a[0:HALF].astype(gl.dtype)
        own[0:HALF] = a[HALF : 2 * HALF] + b[0:HALF]
        own[HALF : 2 * HALF] = a[2 * HALF :] + b[HALF : 2 * HALF]
        gr[n] = b[2 * HALF :].astype(gr.dtype)


def attention(meta, q, k, v, gm, left, right, earlier, off, heads):
    rows, width = q.shape

    def at(n, o):
        return pl.BlockSpec((n, HEAD_DIM), lambda h, s: (0, h + o))

    pair = pl.BlockSpec((2, HALF, HEAD_DIM), lambda h, s: (0, 0, h))
    w = heads * HEAD_DIM
    aliases = {7: 0, 8: 1} if earlier else {}
    return pl.pallas_call(
        attention_kernel,
        name="attention",
        out_shape=[
            SDS((rows, width), BF16),
            SDS((rows, width), BF16),
            SDS((rows, w), F32),
            SDS((rows, w), F32),
            SDS((2, HALF, w), BF16),
            SDS((2, HALF, w), BF16),
        ],
        grid_spec=pltpu.PrefetchScalarGridSpec(
            num_scalar_prefetch=1,
            grid=(heads,),
            in_specs=[at(rows, off)] * 4 + [pair] * 2 + [ANY] * len(earlier),
            out_specs=[at(rows, off)] * 2 + [at(rows, 0)] * 2 + [pair] * 2,
            scratch_shapes=[pltpu.VMEM((rows // HALF, HALF, 3 * HALF), F32)],
        ),
        input_output_aliases=aliases,
        compiler_params=pltpu.CompilerParams(dimension_semantics=("arbitrary",)),
    )(meta, q, k, v, gm, left, right, *earlier)


def join_kernel(dk, dv, low, high, *refs):
    for n, (own, out) in enumerate(zip((dk, dv), refs[-2:])):
        out[0:HALF] = (own[0:HALF] + low[n].astype(F32)).astype(out.dtype)
        out[HALF:] = (own[HALF:] + high[n].astype(F32)).astype(out.dtype)


def join(dk, dv, low, high, earlier, off, width, block=256):
    rows, w = dk.shape
    own = pl.BlockSpec((rows, block), lambda i: (0, i))
    pair = pl.BlockSpec((2, HALF, block), lambda i: (0, 0, i))
    out = pl.BlockSpec((rows, block), lambda i: (0, i + off // block))
    return pl.pallas_call(
        join_kernel,
        name="join",
        out_shape=[SDS((rows, width), BF16)] * 2,
        grid=(w // block,),
        in_specs=[own] * 2 + [pair] * 2 + [ANY] * len(earlier),
        out_specs=[out] * 2,
        input_output_aliases={4: 0, 5: 1} if earlier else {},
    )(dk, dv, low, high, *earlier)


def weight_kernel(core, go, att, keep, send, total):
    total[...] = dot_tn(go[...], att[...])
    n = keep.shape[1] // 2
    for i in range(2):
        mine = pl.multiple_of((2 * i + core[0]) * n, n)
        theirs = pl.multiple_of((2 * i + 1 - core[0]) * n, n)
        keep[0, i * n : (i + 1) * n] = total[pl.ds(mine, n)]
        send[0, i * n : (i + 1) * n] = total[pl.ds(theirs, n)].astype(send.dtype)


def weight_parts(core, go, att, off, heads):
    rows, width = go.shape
    wide = heads * HEAD_DIM
    half = pl.BlockSpec((1, width // 8, wide), lambda y, s: (y, 0, 0))
    return pl.pallas_call(
        weight_kernel,
        name="weight",
        out_shape=[SDS((4, width // 8, wide), F32), SDS((4, width // 8, wide), BF16)],
        grid_spec=pltpu.PrefetchScalarGridSpec(
            num_scalar_prefetch=1,
            grid=(4,),
            in_specs=[
                pl.BlockSpec((rows, width // 4), lambda y, s: (0, y)),
                pl.BlockSpec((rows, wide), lambda y, s: (0, off // heads)),
            ],
            out_specs=[half, half],
            scratch_shapes=[pltpu.VMEM((width // 4, wide), F32)],
        ),
    )(core, go, att)


def part_kernel(y, keep, got, own, *outs):
    k = pl.program_id(0)
    total = keep[0] + got[0].astype(F32)

    @pl.when(k == 0)
    def _():
        own[...] = total

    for n, out in enumerate(outs):

        @pl.when(k == n + 1)
        def _(out=out):
            out[...] = total.astype(out.dtype)


def parted(y, keep, got):
    _, n, wide = keep.shape
    turned = pl.BlockSpec((1, n, wide), lambda k, s: (lax.rem(s[0] + k, 4), 0, 0))
    fixed = pl.BlockSpec((n, wide), lambda k, s: (0, 0))
    return pl.pallas_call(
        part_kernel,
        name="parted",
        out_shape=[SDS((n, wide), F32)] + [SDS((n, wide), BF16)] * 3,
        grid_spec=pltpu.PrefetchScalarGridSpec(
            num_scalar_prefetch=1,
            grid=(4,),
            in_specs=[turned, turned],
            out_specs=[fixed] * 4,
        ),
    )(y, keep, got)


def passed(value, axis, by):
    devices = lax.axis_size(axis)
    pairs = [(i, i + by) for i in range(devices) if 0 <= i + by < devices]
    return lax.ppermute(value, axis, pairs)


def turned(value, axis, by):
    devices = lax.axis_size(axis)
    return lax.ppermute(value, axis, [(i, (i + by) % devices) for i in range(devices)])


def mixed_kernel(place, go, *refs):
    pieces, (out, weight, sems) = refs[:8], refs[8:]
    y, core = place[0], place[1]
    copies = []
    for n, piece in enumerate(pieces):
        side = core if n < 4 else 1 - core
        copies.append(
            pltpu.make_async_copy(
                piece, weight.at[lax.rem(y + 4 - n % 4, 4), :, side], sems.at[n]
            )
        )
    for copy in copies:
        copy.start()
    for copy in copies:
        copy.wait()
    out[...] = dot_nn(go[...], weight[...].reshape(go.shape[1], -1)).astype(out.dtype)


def mixed(place, go, pieces):
    rows, width = go.shape
    whole = pl.BlockSpec((rows, width), lambda i, s: (0, 0))
    return pl.pallas_call(
        mixed_kernel,
        name="mixed",
        out_shape=SDS((rows, width), BF16),
        grid_spec=pltpu.PrefetchScalarGridSpec(
            num_scalar_prefetch=1,
            grid=(1,),
            in_specs=[whole] + [ANY] * 8,
            out_specs=whole,
            scratch_shapes=[
                pltpu.VMEM((4, 2, 2) + pieces[0].shape[1:], BF16),
                pltpu.SemaphoreType.DMA((8,)),
            ],
        ),
    )(place, go, *pieces)


def swapped(value, bit):
    return lax.ppermute(value, "dp", [(i, i ^ bit) for i in range(lax.axis_size("dp"))])


def gathered(shard):
    low = (lax.axis_index("dp") // 2) % 2 == 0
    other = swapped(shard, 2)
    mine = [jnp.stack([jnp.where(low, shard, other), jnp.where(low, other, shard)])]
    for n in (1, 2, 3):
        mine.append(turned(mine[0], "dp", 4 * n))
    theirs = []
    for piece in mine:
        theirs.append(swapped(piece, 1))
    return mine + theirs


def deal_kernel(z, *refs):
    *ins, spread = refs
    own, *outs = ins[-8:]
    ins = ins[:-8]
    n = own.shape[1]
    off = 0
    for chunk in range(0, len(ins), 4):
        first, *rest = ins[chunk : chunk + 4]
        total = first[...]
        for got in rest:
            total = total + got[...].astype(F32)
        wide = total.shape[1]
        for x in range(2):
            for k in range(8):
                row = (x * 8 + k) * n
                spread[x, k, 0:n, off : off + wide] = total[row : row + n]
        off += wide
    for k, out in enumerate((own, *outs)):
        for x in range(2):
            out[x] = spread[x, lax.rem(z[0] + k, 8), 0:n].astype(out.dtype)


def deal(z, parts, width):
    rows = parts[0].shape[0] // 16
    shape = (2, rows, width)
    return pl.pallas_call(
        deal_kernel,
        name="deal",
        out_shape=[SDS(shape, F32)] + [SDS(shape, BF16)] * 7,
        grid_spec=pltpu.PrefetchScalarGridSpec(
            num_scalar_prefetch=1,
            grid=(1,),
            in_specs=[pl.BlockSpec(p.shape, lambda i, s: (0, 0)) for p in parts],
            out_specs=[pl.BlockSpec(shape, lambda i, s: (0, 0, 0))] * 8,
            scratch_shapes=[pltpu.VMEM((2, 8, 16, width), F32)],
        ),
    )(z, *parts)


def quarter_kernel(place, own, *refs):
    gots, outs = refs[:7], refs[7:]
    total = own[...]
    for got in gots:
        total = total + got[...].astype(F32)
    n = outs[0].shape[0]
    quarters = [[total[x, h * n : (h + 1) * n] for h in range(2)] for x in range(2)]
    for k, out in enumerate(outs):
        x, h = place[0] ^ (k // 2), place[1] ^ (k % 2)
        low = jnp.where(h == 0, quarters[0][0], quarters[0][1])
        high = jnp.where(h == 0, quarters[1][0], quarters[1][1])
        out[...] = jnp.where(x == 0, low, high)


def quartered(place, own, gots):
    _, rows, width = own.shape
    whole = pl.BlockSpec(own.shape, lambda i, s: (0, 0, 0))
    part = pl.BlockSpec((rows // 2, width), lambda i, s: (0, 0))
    return pl.pallas_call(
        quarter_kernel,
        name="quarter",
        out_shape=[SDS((rows // 2, width), F32)] * 4,
        grid_spec=pltpu.PrefetchScalarGridSpec(
            num_scalar_prefetch=1, grid=(1,), in_specs=[whole] * 8, out_specs=[part] * 4
        ),
    )(place, own, *gots)


def crossed(value, k):
    count = lax.axis_size("seq")
    pairs = [
        (d * count + s, (d ^ (k // 2 * 2)) * count + (s ^ (k % 2)))
        for d in range(lax.axis_size("dp"))
        for s in range(count)
    ]
    return lax.ppermute(value, ("dp", "seq"), pairs)


CHUNKS = (8, 4)


def step(queries, keys, values, grad_out, out_weight, lengths):
    rows, width = queries.shape
    first_row = lax.axis_index("seq") * rows
    dp = lax.axis_index("dp")
    y, core = dp // 4, dp % 2
    meta = jnp.stack([first_row, lengths[0]]).astype(jnp.int32)
    offs = [sum(CHUNKS[:n]) for n in range(len(CHUNKS))]
    pieces = gathered(out_weight)
    halos = []
    for off, heads in zip(offs, CHUNKS):
        a, b = off * HEAD_DIM, (off + heads) * HEAD_DIM
        tail = jnp.stack([keys[rows - HALF :, a:b], values[rows - HALF :, a:b]])
        head = jnp.stack([keys[:HALF, a:b], values[:HALF, a:b]])
        left = passed(tail, "seq", 1)
        right = passed(head, "seq", -1)
        halos.append((left, right))
    grad_mixed = mixed(jnp.stack([y, core]).astype(jnp.int32), grad_out, pieces)
    earlier, sums, parts = (), [], []
    for (left, right), off, heads in zip(halos, offs, CHUNKS):
        att, dq, dk, dv, gl, gr = attention(
            meta, queries, keys, values, grad_mixed, left, right, earlier, off, heads
        )
        earlier = (att, dq)
        low = passed(gr, "seq", 1)
        high = passed(gl, "seq", -1)
        sums.append((dk, dv, low, high))
        keep, send = weight_parts(core[None], grad_out, att, off, heads)
        got = swapped(send, 1)
        own, *rest = parted(y[None], keep, got)
        gots = []
        for k, part in enumerate(rest):
            gots.append(turned(part, "dp", 4 * (k + 1)))
        parts += [own, *gots]
    seq = lax.axis_index("seq")
    own, *rest = deal((seq // 2)[None], parts, width)
    gots = []
    for k, part in enumerate(rest):
        gots.append(turned(part, "seq", 2 * (k + 1)))
    place = jnp.stack([(dp // 2) % 2, seq % 2]).astype(jnp.int32)
    own, *rest = quartered(place, own, gots)
    for k, part in enumerate(rest):
        own = own + crossed(part, k + 1)
    outs = ()
    for n, off in enumerate(offs):
        outs = tuple(join(*sums[n], outs, off * HEAD_DIM, width))
    return dq, outs[0], outs[1], own


def solution(mesh):
    rows = P(("dp", "seq"), None)
    return jax.shard_map(
        step,
        mesh=mesh,
        in_specs=(rows, rows, rows, rows, P("dp", None), P("dp")),
        out_specs=(rows, rows, rows, rows),
        check_vma=False,
    )
```

time: 342 us -> 273 us (0.80); the launches traced: 341 us -> 269 us
  waiting for transfers between devices: 183 us -> 99.9 us
  Pallas kernels: 27.1 us -> 69.8 us
  other arithmetic: 39.5 us -> 5.78 us
  starting transfers between devices: 51.1 us -> 82.9 us
  between operations: 15 us -> 1.6 us
  matrix products: 12.5 us -> 0 us
  local copies, waits for them, and re-layouts: 12.9 us -> 8.54 us
    all_gather x1 -> x0, waiting for transfers between devices: 65.6 us -> none  [shards(): weight = lax.all_gather(out_weight, 'dp', axis=0, tiled=True)]
    pallas_call x1 -> x11, Pallas kernels: 27.1 us -> 69.8 us  [the longest x2 29.9 us: attention(): pl.pallas_call(attention_kernel, name='attention', out_shape=[SDS((rows,...]
    ppermute x8 -> x26, starting transfers between devices: 22.4 us -> 59.1 us  [the longest x16 49.2 us: turned(): lax.ppermute(value, axis, [(i, (i + by) % devices) for i in range(devices)])]
    add x8 -> x1, other arithmetic: 21.3 us -> 0.63 us  [step(): own = own + crossed(part, k + 1)]
    convert_element_type x10 -> x0, other arithmetic: 17.6 us -> none  [the longest x8 12.4 us: halved(): sent = jnp.where(mine, low, high).astype(jnp.bfloat16)]
    ppermute x8, waiting for transfers between devices: 39.6 us -> 25.4 us  [passed(): return lax.ppermute(value, axis, pairs)]
    dot_general x2 -> x0, matrix products: 12.5 us -> none  [the longest x1 6.53 us: shards(): lax.dot_general(grad_out, att, (((0,), (0,)), ((), ())), preferred_elemen...]
    slice x3 -> x0, local copies, waits for them, and re-layouts: 9.03 us -> none  [the longest x1 5.13 us: halved(): high = lax.slice_in_dim(value, 1, 2, axis=dim)]
  transfers between devices with their start and end apart: 17 -> 34, of which waited for: 9 -> 17; matrix products, arithmetic and copies ran while one was open for 5% -> 3% of each run, Pallas kernels for 0% -> 17%
where the time goes in v2:
time: 273 us; the launch traced here: 269 us
  waiting for transfers between devices  99.9 us (37%)
  starting transfers between devices  82.9 us (30%)
  Pallas kernels  69.8 us (26%)
  local copies, waits for them, and re-layouts  8.54 us (3%)
  other arithmetic  5.78 us (2%)
    ppermute x16, waiting for transfers between devices, turned(): lax.ppermute(value, axis, [(i, (i + by) % devices) for i in range(devices)])  63.6 us
    ppermute x16, starting transfers between devices, turned(): lax.ppermute(value, axis, [(i, (i + by) % devices) for i in range(devices)])  49.2 us
    pallas_call x2, Pallas kernels, attention(): pl.pallas_call(attention_kernel, name='attention', out_shape=[SDS((rows,...  29.9 us
    ppermute x8, waiting for transfers between devices, passed(): return lax.ppermute(value, axis, pairs)  25.4 us
    ppermute x8, starting transfers between devices, passed(): return lax.ppermute(value, axis, pairs)  23.9 us
    ppermute x7, waiting for transfers between devices, swapped(): lax.ppermute(value, 'dp', [(i, i ^ bit) for i in range(lax.axis_size('dp'...  10.9 us
    pallas_call x2, Pallas kernels, weight_parts(): pl.pallas_call(weight_kernel, name='weight', out_shape=[SDS((4, width //...  10.6 us
    ppermute x3, starting transfers between devices, crossed(): return lax.ppermute(value, ('dp', 'seq'), pairs)  9.1 us
  transfers between devices with their start and end apart: 34, of which 17 were waited for; matrix products, arithmetic and copies ran while one was open for 3% of the time, Pallas kernels for 17%

profile of v2, /device:TPU:18, one launch (start us, length us, event | category | flops | bytes accessed | tf_op | source)
XLA Modules:
  0.0 268.6 jit_solution(6485537860266614224)
XLA Ops:
  1.3 8.4 %collective-permute-done = bf16[96,1536]{1,0:T(8,128)(2,1)S(1)} collective-permute-done((bf16[96,1536]{1,0:T(8,128)(2,1)}, bf16[96,1536]{1,0:T(8,128)(2,1)S(1)}, u32[]{:S(2)}, u32[]{:S(2)}) %collective-permute-start) | collective-permute-done | bytes 294944 | tf_op jit(solution)/shard_map/ppermute | solution.py:246
  13.5 4.1 %collective-permute-start.10 = (bf16[2,256,1024]{2,1,0:T(8,128)(2,1)}, bf16[2,256,1024]{2,1,0:T(8,128)(2,1)S(1)}, u32[]{:S(2)}, u32[]{:S(2)}) collective-permute-start(bf16[2,256,1024]{2,1,0:T(8,128)(2,1)} %pad_maximum_fusion), channel_id=1, source_target_pairs={{0,1},{1,2},{2,3},{3,4},{4,5},{5,6},{6,7},{7,8},{8,9},{9,10},{10,1... | collective-permute-start | bytes 3145736 | tf_op jit(solution)/shard_map/ppermute | solution.py:199
  23.3 10.6 %collective-permute-done.3.refs_3_ = bf16[2,96,1536]{2,1,0:T(8,128)(2,1)} collective-permute-done((bf16[2,96,1536]{2,1,0:T(8,128)(2,1)S(1)}, bf16[2,96,1536]{2,1,0:T(8,128)(2,1)}, u32[]{:S(2)}, u32[]{:S(2)}) %collective-permute-start.3) | collective-permute-done | bytes 589856 | tf_op jit(solution)/shard_map/ppermute | solution.py:204
  35.9 11.5 %collective-permute-done.1.refs_1_ = bf16[2,96,1536]{2,1,0:T(8,128)(2,1)} collective-permute-done((bf16[2,96,1536]{2,1,0:T(8,128)(2,1)S(1)}, bf16[2,96,1536]{2,1,0:T(8,128)(2,1)}, u32[]{:S(2)}, u32[]{:S(2)}) %collective-permute-start.1) | collective-permute-done | bytes 589856 | tf_op jit(solution)/shard_map/ppermute | solution.py:204
  51.2 8.2 %mixed.1.gm = bf16[512,1536]{1,0:T(8,128)(2,1)} custom-call(s32[2]{0:T(128)} %pad_add_fusion.1.place, bf16[512,1536]{1,0:T(8,128)(2,1)} %go.5, bf16[2,96,1536]{2,1,0:T(8,128)(2,1)} %copy-done.1, bf16[2,96,1536]{2,1,0:T(8,128)(2,1)} %collective-permute-done.1.refs_1_, bf16[2,96,1536]{2,1,0:T(8,128)(2,1)} %collective-permute-done.2.refs_2_, ...), custom_call_target="tpu_custom_call" | custom-call | tf_op jit(solution)/shard_map/mixed/pallas_call | solution.py:228
  64.3 19.0 %attention.2 = (bf16[512,1536]{1,0:T(8,128)(2,1)}, bf16[512,1536]{1,0:T(8,128)(2,1)}, f32[512,1024]{1,0:T(8,128)}, f32[512,1024]{1,0:T(8,128)}, bf16[2,256,1024]...) custom-call(s32[2]{0:T(128)} %pad_add_fusion.meta, bf16[512,1536]{1,0:T(8,128)(2,1)} %q.3, bf16[512,1536]{1,0:T(8,128)(2,1)} %k.3, ...), custom_call_target="tpu_custom_call" | custom-call | tf_op jit(solution)/shard_map/attention/pallas_call | solution.py:88
  83.2 5.9 %weight.2 = (f32[4,192,1024]{2,1,0:T(8,128)}, bf16[4,192,1024]{2,1,0:T(8,128)(2,1)}) custom-call(s32[1]{0:T(128)} %bitcast.2.core, bf16[512,1536]{1,0:T(8,128)(2,1)} %go.5, bf16[512,1536]{1,0:T(8,128)(2,1)} %get-tuple-element.44.refs_0_.att), custom_call_target="tpu_custom_call" | custom-call | tf_op jit(solution)/shard_map/weight/pallas_call | solution.py:147
  89.2 5.8 %collective-permute-start.8 = (bf16[2,256,512]{2,1,0:T(8,128)(2,1)S(1)}, bf16[2,256,512]{2,1,0:T(8,128)(2,1)S(1)}, u32[]{:S(2)}, u32[]{:S(2)}) collective-permute-start(bf16[2,256,512]{2,1,0:T(8,128)(2,1)S(1)} %pad_maximum_fusion.3), channel_id=1, source_target_pairs={{0,1},{1,2},{2,3},{3,4},{4,5},{5,6},{6,7},{7,8},{8,9},{9,10},{10,1... | collective-permute-start | bytes 1572872 | tf_op jit(solution)/shard_map/ppermute | solution.py:199
  96.5 21.5 %collective-permute-done.8.left = bf16[2,256,512]{2,1,0:T(8,128)(2,1)S(1)} collective-permute-done((bf16[2,256,512]{2,1,0:T(8,128)(2,1)S(1)}, bf16[2,256,512]{2,1,0:T(8,128)(2,1)S(1)}, u32[]{:S(2)}, u32[]{:S(2)}) %collective-permute-start.8) | collective-permute-done | bytes 524320 | tf_op jit(solution)/shard_map/ppermute | solution.py:199
  119.0 11.0 %attention.3 = (bf16[512,1536]{1,0:T(8,128)(2,1)}, bf16[512,1536]{1,0:T(8,128)(2,1)}, f32[512,512]{1,0:T(8,128)}, f32[512,512]{1,0:T(8,128)}, bf16[2,256,512]{2,...) custom-call(s32[2]{0:T(128)} %pad_add_fusion.meta, bf16[512,1536]{1,0:T(8,128)(2,1)} %q.3, ...), custom_call_target="tpu_custom_call", output_to_operand_aliasing={{0}: (7, {}), {1}: (8, {})} | custom-call | tf_op jit(solution)/shard_map/attention/pallas_call | solution.py:88
  130.0 4.7 %weight.3 = (f32[4,192,512]{2,1,0:T(8,128)}, bf16[4,192,512]{2,1,0:T(8,128)(2,1)}) custom-call(s32[1]{0:T(128)} %bitcast.2.core, bf16[512,1536]{1,0:T(8,128)(2,1)} %go.5, bf16[512,1536]{1,0:T(8,128)(2,1)} %get-tuple-element.65.att), custom_call_target="tpu_custom_call" | custom-call | tf_op jit(solution)/shard_map/weight/pallas_call | solution.py:147
  144.5 5.9 %collective-permute-start.14 = (bf16[2,256,1024]{2,1,0:T(8,128)(2,1)}, bf16[2,256,1024]{2,1,0:T(8,128)(2,1)S(1)}, u32[]{:S(2)}, u32[]{:S(2)}) collective-permute-start(bf16[2,256,1024]{2,1,0:T(8,128)(2,1)} %get-tuple-element.53), channel_id=1, source_target_pairs={{0,1},{1,2},{2,3},{3,4},{4,5},{5,6},{6,7},{7,8},{8,9},{9,10},{10,1... | collective-permute-start | bytes 3145736 | tf_op jit(solution)/shard_map/ppermute | solution.py:199
  151.8 4.5 %parted.2 = (f32[192,1024]{1,0:T(8,128)}, bf16[192,1024]{1,0:T(8,128)(2,1)}, bf16[192,1024]{1,0:T(8,128)(2,1)}, bf16[192,1024]{1,0:T(8,128)(2,1)}) custom-call(s32[1]{0:T(128)} %bitcast.1.y, f32[4,192,1024]{2,1,0:T(8,128)} %get-tuple-element.59.keep, bf16[4,192,1024]{2,1,0:T(8,128)(2,1)} %copy-done.2), custom_call_target="tpu_custom_call" | custom-call | tf_op jit(solution)/shard_map/parted/pallas_call | solution.py:183
  162.2 5.9 %collective-permute-done.17.refs_1_ = bf16[192,1024]{1,0:T(8,128)(2,1)S(1)} collective-permute-done((bf16[192,1024]{1,0:T(8,128)(2,1)}, bf16[192,1024]{1,0:T(8,128)(2,1)S(1)}, u32[]{:S(2)}, u32[]{:S(2)}) %collective-permute-start.17) | collective-permute-done | bytes 393248 | tf_op jit(solution)/shard_map/ppermute | solution.py:204
  168.0 8.8 %collective-permute-done.18.refs_2_ = bf16[192,1024]{1,0:T(8,128)(2,1)S(1)} collective-permute-done((bf16[192,1024]{1,0:T(8,128)(2,1)}, bf16[192,1024]{1,0:T(8,128)(2,1)S(1)}, u32[]{:S(2)}, u32[]{:S(2)}) %collective-permute-start.18) | collective-permute-done | bytes 393248 | tf_op jit(solution)/shard_map/ppermute | solution.py:204
  181.5 5.2 %collective-permute-start.24 = (bf16[2,12,1536]{2,1,0:T(8,128)(2,1)}, bf16[2,12,1536]{2,1,0:T(8,128)(2,1)S(1)}, u32[]{:S(2)}, u32[]{:S(2)}) collective-permute-start(bf16[2,12,1536]{2,1,0:T(8,128)(2,1)} %get-tuple-element.73), channel_id=1, source_target_pairs={{0,2},{1,3},{2,4},{3,5},{4,6},{5,7},{6,8},{7,9},{8,10},{9,11},{10,... | collective-permute-start | bytes 221192 | tf_op jit(solution)/shard_map/ppermute | solution.py:204
  193.5 4.9 %collective-permute-start.25 = (bf16[2,12,1536]{2,1,0:T(8,128)(2,1)}, bf16[2,12,1536]{2,1,0:T(8,128)(2,1)S(1)}, u32[]{:S(2)}, u32[]{:S(2)}) collective-permute-start(bf16[2,12,1536]{2,1,0:T(8,128)(2,1)} %get-tuple-element.74), channel_id=1, source_target_pairs={{0,4},{1,5},{2,6},{3,7},{4,8},{5,9},{6,10},{7,11},{8,12},{9,13},{1... | collective-permute-start | bytes 221192 | tf_op jit(solution)/shard_map/ppermute | solution.py:204
  198.3 6.0 %collective-permute-done.25.refs_1_ = bf16[2,12,1536]{2,1,0:T(8,128)(2,1)S(1)} collective-permute-done((bf16[2,12,1536]{2,1,0:T(8,128)(2,1)}, bf16[2,12,1536]{2,1,0:T(8,128)(2,1)S(1)}, u32[]{:S(2)}, u32[]{:S(2)}) %collective-permute-start.25) | collective-permute-done | bytes 73760 | tf_op jit(solution)/shard_map/ppermute | solution.py:204
  204.3 6.0 %collective-permute-start.26 = (bf16[2,12,1536]{2,1,0:T(8,128)(2,1)}, bf16[2,12,1536]{2,1,0:T(8,128)(2,1)S(1)}, u32[]{:S(2)}, u32[]{:S(2)}) collective-permute-start(bf16[2,12,1536]{2,1,0:T(8,128)(2,1)} %get-tuple-element.75), channel_id=1, source_target_pairs={{0,6},{1,7},{2,8},{3,9},{4,10},{5,11},{6,12},{7,13},{8,14},{9,15},... | collective-permute-start | bytes 221192 | tf_op jit(solution)/shard_map/ppermute | solution.py:204
  214.0 8.0 %collective-permute-start.27 = (bf16[2,12,1536]{2,1,0:T(8,128)(2,1)}, bf16[2,12,1536]{2,1,0:T(8,128)(2,1)S(1)}, u32[]{:S(2)}, u32[]{:S(2)}) collective-permute-start(bf16[2,12,1536]{2,1,0:T(8,128)(2,1)} %get-tuple-element.76), channel_id=1, source_target_pairs={{0,8},{1,9},{2,10},{3,11},{4,12},{5,13},{6,14},{7,15},{8,0},{9,1},... | collective-permute-start | bytes 221192 | tf_op jit(solution)/shard_map/ppermute | solution.py:204
  225.8 4.6 %collective-permute-start.28 = (bf16[2,12,1536]{2,1,0:T(8,128)(2,1)}, bf16[2,12,1536]{2,1,0:T(8,128)(2,1)S(1)}, u32[]{:S(2)}, u32[]{:S(2)}) collective-permute-start(bf16[2,12,1536]{2,1,0:T(8,128)(2,1)} %get-tuple-element.77), channel_id=1, source_target_pairs={{0,10},{1,11},{2,12},{3,13},{4,14},{5,15},{6,0},{7,1},{8,2},{9,3},... | collective-permute-start | bytes 221192 | tf_op jit(solution)/shard_map/ppermute | solution.py:204
  239.6 5.1 %collective-permute-start.30 = (bf16[2,12,1536]{2,1,0:T(8,128)(2,1)}, bf16[2,12,1536]{2,1,0:T(8,128)(2,1)S(1)}, u32[]{:S(2)}, u32[]{:S(2)}) collective-permute-start(bf16[2,12,1536]{2,1,0:T(8,128)(2,1)} %get-tuple-element.79), channel_id=1, source_target_pairs={{0,14},{1,15},{2,0},{3,1},{4,2},{5,3},{6,4},{7,5},{8,6},{9,7},{10,... | collective-permute-start | bytes 221192 | tf_op jit(solution)/shard_map/ppermute | solution.py:204
  250.5 7.5 %collective-permute-start.31 = (f32[6,1536]{1,0:T(8,128)}, f32[6,1536]{1,0:T(8,128)S(1)}, u32[]{:S(2)}, u32[]{:S(2)}) collective-permute-start(f32[6,1536]{1,0:T(8,128)} %get-tuple-element.81), channel_id=1, source_target_pairs={{0,1},{1,0},{2,3},{3,2},{4,5},{5,4},{6,7},{7,6},{8,9},{9,8},{10,11... | collective-permute-start | bytes 110600 | tf_op jit(solution)/shard_map/ppermute | solution.py:335
  259.6 4.6 %join.2 = (bf16[512,1536]{1,0:T(8,128)(2,1)}, bf16[512,1536]{1,0:T(8,128)(2,1)}) custom-call(f32[512,1024]{1,0:T(8,128)} %get-tuple-element.51.dk, f32[512,1024]{1,0:T(8,128)} %get-tuple-element.52.dv, bf16[2,256,1024]{2,1,0:T(8,128)(2,1)} %copy-done.4, bf16[2,256,1024]{2,1,0:T(8,128)(2,1)} %collective-permute-done.15.high), custom_call_target="tpu_custom_call" | custom-call | tf_op jit(solution)/shard_map/join/pallas_call | solution.py:122
  (119 shorter events, 79.5 us)
Async XLA Ops:
  10.8 11.3 %collective-permute-start.4 = (bf16[2,96,1536]{2,1,0:T(8,128)(2,1)S(1)}, bf16[2,96,1536]{2,1,0:T(8,128)(2,1)S(1)}, u32[]{:S(2)}, u32[]{:S(2)}) collective-permute-start(bf16[2,96,1536]{2,1,0:T(8,128)(2,1)S(1)} %pad_maximum_fusion.2.refs_0_), channel_id=1, source_target_pairs={{0,16},{16,0},{32,48},{48,32},{64,80},{80,64},{96,112},{112,96},{1... | collective-permute-start | bytes 1769480 | tf_op jit(solution)/shard_map/ppermute | solution.py:246
  13.5 49.8 %collective-permute-start.10 = (bf16[2,256,1024]{2,1,0:T(8,128)(2,1)}, bf16[2,256,1024]{2,1,0:T(8,128)(2,1)S(1)}, u32[]{:S(2)}, u32[]{:S(2)}) collective-permute-start(bf16[2,256,1024]{2,1,0:T(8,128)(2,1)} %pad_maximum_fusion), channel_id=1, source_target_pairs={{0,1},{1,2},{2,3},{3,4},{4,5},{5,6},{6,7},{7,8},{8,9},{9,10},{10,1... | collective-permute-start | bytes 3145736 | tf_op jit(solution)/shard_map/ppermute | solution.py:199
  17.6 16.4 %collective-permute-start.3 = (bf16[2,96,1536]{2,1,0:T(8,128)(2,1)S(1)}, bf16[2,96,1536]{2,1,0:T(8,128)(2,1)}, u32[]{:S(2)}, u32[]{:S(2)}) collective-permute-start(bf16[2,96,1536]{2,1,0:T(8,128)(2,1)S(1)} %pad_maximum_fusion.2.refs_0_), channel_id=1, source_target_pairs={{0,192},{16,208},{32,224},{48,240},{64,0},{80,16},{96,32},{112,48}... | collective-permute-start | bytes 1769480 | tf_op jit(solution)/shard_map/ppermute | solution.py:204
  18.1 17.9 %collective-permute-start.2 = (bf16[2,96,1536]{2,1,0:T(8,128)(2,1)S(1)}, bf16[2,96,1536]{2,1,0:T(8,128)(2,1)}, u32[]{:S(2)}, u32[]{:S(2)}) collective-permute-start(bf16[2,96,1536]{2,1,0:T(8,128)(2,1)S(1)} %pad_maximum_fusion.2.refs_0_), channel_id=1, source_target_pairs={{0,128},{16,144},{32,160},{48,176},{64,192},{80,208},{96,224},{112... | collective-permute-start | bytes 1769480 | tf_op jit(solution)/shard_map/ppermute | solution.py:204
  21.0 26.4 %collective-permute-start.1 = (bf16[2,96,1536]{2,1,0:T(8,128)(2,1)S(1)}, bf16[2,96,1536]{2,1,0:T(8,128)(2,1)}, u32[]{:S(2)}, u32[]{:S(2)}) collective-permute-start(bf16[2,96,1536]{2,1,0:T(8,128)(2,1)S(1)} %pad_maximum_fusion.2.refs_0_), channel_id=1, source_target_pairs={{0,64},{16,80},{32,96},{48,112},{64,128},{80,144},{96,160},{112,17... | collective-permute-start | bytes 1769480 | tf_op jit(solution)/shard_map/ppermute | solution.py:204
  22.1 41.2 %collective-permute-start.11 = (bf16[2,256,1024]{2,1,0:T(8,128)(2,1)}, bf16[2,256,1024]{2,1,0:T(8,128)(2,1)}, u32[]{:S(2)}, u32[]{:S(2)}) collective-permute-start(bf16[2,256,1024]{2,1,0:T(8,128)(2,1)} %pad_maximum_fusion.1), channel_id=1, source_target_pairs={{1,0},{2,1},{3,2},{4,3},{5,4},{6,5},{7,6},{8,7},{9,8},{10,9},{11,1... | collective-permute-start | bytes 3145736 | tf_op jit(solution)/shard_map/ppermute | solution.py:199
  33.9 17.2 %collective-permute-start.7 = (bf16[2,96,1536]{2,1,0:T(8,128)(2,1)}, bf16[2,96,1536]{2,1,0:T(8,128)(2,1)}, u32[]{:S(2)}, u32[]{:S(2)}) collective-permute-start(bf16[2,96,1536]{2,1,0:T(8,128)(2,1)} %collective-permute-done.3.refs_3_), channel_id=1, source_target_pairs={{0,16},{16,0},{32,48},{48,32},{64,80},{80,64},{96,112},{112,96},{1... | collective-permute-start | bytes 1769480 | tf_op jit(solution)/shard_map/ppermute | solution.py:246
  35.9 15.2 %collective-permute-start.6 = (bf16[2,96,1536]{2,1,0:T(8,128)(2,1)}, bf16[2,96,1536]{2,1,0:T(8,128)(2,1)}, u32[]{:S(2)}, u32[]{:S(2)}) collective-permute-start(bf16[2,96,1536]{2,1,0:T(8,128)(2,1)} %collective-permute-done.2.refs_2_), channel_id=1, source_target_pairs={{0,16},{16,0},{32,48},{48,32},{64,80},{80,64},{96,112},{112,96},{1... | collective-permute-start | bytes 1769480 | tf_op jit(solution)/shard_map/ppermute | solution.py:246
  89.1 61.3 %collective-permute-start.16 = (bf16[4,192,1024]{2,1,0:T(8,128)(2,1)}, bf16[4,192,1024]{2,1,0:T(8,128)(2,1)S(1)}, u32[]{:S(2)}, u32[]{:S(2)}) collective-permute-start(bf16[4,192,1024]{2,1,0:T(8,128)(2,1)} %get-tuple-element.60), channel_id=1, source_target_pairs={{0,16},{16,0},{32,48},{48,32},{64,80},{80,64},{96,112},{112,96},{1... | collective-permute-start | bytes 4718600 | tf_op jit(solution)/shard_map/ppermute | solution.py:246
  89.2 28.9 %collective-permute-start.8 = (bf16[2,256,512]{2,1,0:T(8,128)(2,1)S(1)}, bf16[2,256,512]{2,1,0:T(8,128)(2,1)S(1)}, u32[]{:S(2)}, u32[]{:S(2)}) collective-permute-start(bf16[2,256,512]{2,1,0:T(8,128)(2,1)S(1)} %pad_maximum_fusion.3), channel_id=1, source_target_pairs={{0,1},{1,2},{2,3},{3,4},{4,5},{5,6},{6,7},{7,8},{8,9},{9,10},{10,1... | collective-permute-start | bytes 1572872 | tf_op jit(solution)/shard_map/ppermute | solution.py:199
  95.1 23.0 %collective-permute-start.9 = (bf16[2,256,512]{2,1,0:T(8,128)(2,1)S(1)}, bf16[2,256,512]{2,1,0:T(8,128)(2,1)S(1)}, u32[]{:S(2)}, u32[]{:S(2)}) collective-permute-start(bf16[2,256,512]{2,1,0:T(8,128)(2,1)S(1)} %pad_maximum_fusion.4), channel_id=1, source_target_pairs={{1,0},{2,1},{3,2},{4,3},{5,4},{6,5},{7,6},{8,7},{9,8},{10,9},{11,1... | collective-permute-start | bytes 1572872 | tf_op jit(solution)/shard_map/ppermute | solution.py:199
  141.5 14.8 %collective-permute-start.21 = (bf16[192,512]{1,0:T(8,128)(2,1)}, bf16[192,512]{1,0:T(8,128)(2,1)S(1)}, u32[]{:S(2)}, u32[]{:S(2)}) collective-permute-start(bf16[192,512]{1,0:T(8,128)(2,1)} %get-tuple-element.69), channel_id=1, source_target_pairs={{0,64},{16,80},{32,96},{48,112},{64,128},{80,144},{96,160},{112,17... | collective-permute-start | bytes 589832 | tf_op jit(solution)/shard_map/ppermute | solution.py:204
  142.8 14.7 %collective-permute-start.22 = (bf16[192,512]{1,0:T(8,128)(2,1)}, bf16[192,512]{1,0:T(8,128)(2,1)S(1)}, u32[]{:S(2)}, u32[]{:S(2)}) collective-permute-start(bf16[192,512]{1,0:T(8,128)(2,1)} %get-tuple-element.70), channel_id=1, source_target_pairs={{0,128},{16,144},{32,160},{48,176},{64,192},{80,208},{96,224},{112... | collective-permute-start | bytes 589832 | tf_op jit(solution)/shard_map/ppermute | solution.py:204
  143.4 16.8 %collective-permute-start.23 = (bf16[192,512]{1,0:T(8,128)(2,1)}, bf16[192,512]{1,0:T(8,128)(2,1)S(1)}, u32[]{:S(2)}, u32[]{:S(2)}) collective-permute-start(bf16[192,512]{1,0:T(8,128)(2,1)} %get-tuple-element.71), channel_id=1, source_target_pairs={{0,192},{16,208},{32,224},{48,240},{64,0},{80,16},{96,32},{112,48}... | collective-permute-start | bytes 589832 | tf_op jit(solution)/shard_map/ppermute | solution.py:204
  144.5 113.6 %collective-permute-start.14 = (bf16[2,256,1024]{2,1,0:T(8,128)(2,1)}, bf16[2,256,1024]{2,1,0:T(8,128)(2,1)S(1)}, u32[]{:S(2)}, u32[]{:S(2)}) collective-permute-start(bf16[2,256,1024]{2,1,0:T(8,128)(2,1)} %get-tuple-element.53), channel_id=1, source_target_pairs={{0,1},{1,2},{2,3},{3,4},{4,5},{5,6},{6,7},{7,8},{8,9},{9,10},{10,1... | collective-permute-start | bytes 3145736 | tf_op jit(solution)/shard_map/ppermute | solution.py:199
  150.4 109.2 %collective-permute-start.15 = (bf16[2,256,1024]{2,1,0:T(8,128)(2,1)}, bf16[2,256,1024]{2,1,0:T(8,128)(2,1)}, u32[]{:S(2)}, u32[]{:S(2)}) collective-permute-start(bf16[2,256,1024]{2,1,0:T(8,128)(2,1)} %get-tuple-element.54), channel_id=1, source_target_pairs={{1,0},{2,1},{3,2},{4,3},{5,4},{6,5},{7,6},{8,7},{9,8},{10,9},{11,1... | collective-permute-start | bytes 3145736 | tf_op jit(solution)/shard_map/ppermute | solution.py:199
  156.3 11.8 %collective-permute-start.17 = (bf16[192,1024]{1,0:T(8,128)(2,1)}, bf16[192,1024]{1,0:T(8,128)(2,1)S(1)}, u32[]{:S(2)}, u32[]{:S(2)}) collective-permute-start(bf16[192,1024]{1,0:T(8,128)(2,1)} %get-tuple-element.62), channel_id=1, source_target_pairs={{0,64},{16,80},{32,96},{48,112},{64,128},{80,144},{96,160},{112,17... | collective-permute-start | bytes 1179656 | tf_op jit(solution)/shard_map/ppermute | solution.py:204
  157.5 19.4 %collective-permute-start.18 = (bf16[192,1024]{1,0:T(8,128)(2,1)}, bf16[192,1024]{1,0:T(8,128)(2,1)S(1)}, u32[]{:S(2)}, u32[]{:S(2)}) collective-permute-start(bf16[192,1024]{1,0:T(8,128)(2,1)} %get-tuple-element.63), channel_id=1, source_target_pairs={{0,128},{16,144},{32,160},{48,176},{64,192},{80,208},{96,224},{112... | collective-permute-start | bytes 1179656 | tf_op jit(solution)/shard_map/ppermute | solution.py:204
  160.2 17.4 %collective-permute-start.19 = (bf16[192,1024]{1,0:T(8,128)(2,1)}, bf16[192,1024]{1,0:T(8,128)(2,1)S(1)}, u32[]{:S(2)}, u32[]{:S(2)}) collective-permute-start(bf16[192,1024]{1,0:T(8,128)(2,1)} %get-tuple-element.64), channel_id=1, source_target_pairs={{0,192},{16,208},{32,224},{48,240},{64,0},{80,16},{96,32},{112,48}... | collective-permute-start | bytes 1179656 | tf_op jit(solution)/shard_map/ppermute | solution.py:204
  181.5 11.9 %collective-permute-start.24 = (bf16[2,12,1536]{2,1,0:T(8,128)(2,1)}, bf16[2,12,1536]{2,1,0:T(8,128)(2,1)S(1)}, u32[]{:S(2)}, u32[]{:S(2)}) collective-permute-start(bf16[2,12,1536]{2,1,0:T(8,128)(2,1)} %get-tuple-element.73), channel_id=1, source_target_pairs={{0,2},{1,3},{2,4},{3,5},{4,6},{5,7},{6,8},{7,9},{8,10},{9,11},{10,... | collective-permute-start | bytes 221192 | tf_op jit(solution)/shard_map/ppermute | solution.py:204
  186.7 77.6 %collective-permute-start.12 = (bf16[2,256,512]{2,1,0:T(8,128)(2,1)}, bf16[2,256,512]{2,1,0:T(8,128)(2,1)S(1)}, u32[]{:S(2)}, u32[]{:S(2)}) collective-permute-start(bf16[2,256,512]{2,1,0:T(8,128)(2,1)} %get-tuple-element.49), channel_id=1, source_target_pairs={{0,1},{1,2},{2,3},{3,4},{4,5},{5,6},{6,7},{7,8},{8,9},{9,10},{10,1... | collective-permute-start | bytes 1572872 | tf_op jit(solution)/shard_map/ppermute | solution.py:199
  189.4 74.9 %collective-permute-start.13 = (bf16[2,256,512]{2,1,0:T(8,128)(2,1)}, bf16[2,256,512]{2,1,0:T(8,128)(2,1)S(1)}, u32[]{:S(2)}, u32[]{:S(2)}) collective-permute-start(bf16[2,256,512]{2,1,0:T(8,128)(2,1)} %get-tuple-element.50), channel_id=1, source_target_pairs={{1,0},{2,1},{3,2},{4,3},{5,4},{6,5},{7,6},{8,7},{9,8},{10,9},{11,1... | collective-permute-start | bytes 1572872 | tf_op jit(solution)/shard_map/ppermute | solution.py:199
  214.0 11.7 %collective-permute-start.27 = (bf16[2,12,1536]{2,1,0:T(8,128)(2,1)}, bf16[2,12,1536]{2,1,0:T(8,128)(2,1)S(1)}, u32[]{:S(2)}, u32[]{:S(2)}) collective-permute-start(bf16[2,12,1536]{2,1,0:T(8,128)(2,1)} %get-tuple-element.76), channel_id=1, source_target_pairs={{0,8},{1,9},{2,10},{3,11},{4,12},{5,13},{6,14},{7,15},{8,0},{9,1},... | collective-permute-start | bytes 221192 | tf_op jit(solution)/shard_map/ppermute | solution.py:204
  250.5 17.4 %collective-permute-start.31 = (f32[6,1536]{1,0:T(8,128)}, f32[6,1536]{1,0:T(8,128)S(1)}, u32[]{:S(2)}, u32[]{:S(2)}) collective-permute-start(f32[6,1536]{1,0:T(8,128)} %get-tuple-element.81), channel_id=1, source_target_pairs={{0,1},{1,0},{2,3},{3,2},{4,5},{5,4},{6,7},{7,6},{8,9},{9,8},{10,11... | collective-permute-start | bytes 110600 | tf_op jit(solution)/shard_map/ppermute | solution.py:335
  (36 other events, 381.4 us)

commit v3 on v2

--- a/solution.py
+++ b/solution.py
@@ -45,46 +45,71 @@
             ok = (c >= r) & (c < r + 2 * HALF) & (u >= 0) & (u < length)
             bias[b] = jnp.where(ok, 0.0, -1e30)
 
-    k_all = [left[0], k[0:HALF], k[HALF : 2 * HALF], right[0]]
-    v_all = [left[1], v[0:HALF], v[HALF : 2 * HALF], right[1]]
-    dks, dvs = [], []
-    for b in range(rows // HALF):
-        lo, hi = b * HALF, (b + 1) * HALF
-        qb, gb = q[lo:hi], gm[lo:hi]
-        kc = jnp.concatenate(k_all[b : b + 3], axis=0)
-        vc = jnp.concatenate(v_all[b : b + 3], axis=0)
+    def products(cols, b):
+        def window(n, own, ends):
+            low = ends[0][n, :, cols] if b == 0 else own[0:HALF, cols]
+            high = own[HALF:, cols] if b == 0 else ends[1][n, :, cols]
+            middle = own[0:HALF, cols] if b == 0 else own[HALF:, cols]
+            return jnp.concatenate([low, middle, high], axis=0)
+
+        at = slice(b * HALF, (b + 1) * HALF)
+        qb, gb = q[at, cols], gm[at, cols]
+        kc, vc = window(0, k, (left, right)), window(1, v, (left, right))
         s = dot_nt(qb, kc) + bias[b]
-        dp = dot_nt(gb, vc)
+        return cols, b, qb, gb, kc, vc, s, dot_nt(gb, vc)
+
+    def softmax(cols, b, qb, gb, kc, vc, s, dp):
         m = jnp.max(s, axis=1, keepdims=True)
         e = jnp.exp2((s - m) * (scale * LOG2E))
-        pos = first_row + lo + lax.broadcasted_iota(jnp.int32, (HALF, 1), 0)
+        pos = first_row + b * HALF + lax.broadcasted_iota(jnp.int32, (HALF, 1), 0)
         total = jnp.maximum(jnp.sum(e, axis=1, keepdims=True), 1.0)
-        inv = jnp.where(pos < length, 1.0 / total, 0.0)
-        p = e * inv
-        pb = p.astype(BF16)
-        att[lo:hi] = dot_nn(pb, vc).astype(att.dtype)
+        p = e * jnp.where(pos < length, 1.0 / total, 0.0)
         delta = jnp.sum(p * dp, axis=1, keepdims=True)
-        ds = (p * (dp - delta) * scale).astype(BF16)
-        dq[lo:hi] = dot_nn(ds, kc).astype(dq.dtype)
-        dks.append(dot_tn(ds, qb))
-        dvs.append(dot_tn(pb, gb))
-    for n, (parts, own) in enumerate(((dks, dk), (dvs, dv))):
-        a, b = parts
-        gl[n] = a[0:HALF].astype(gl.dtype)
-        own[0:HALF] = a[HALF : 2 * HALF] + b[0:HALF]
-        own[HALF : 2 * HALF] = a[2 * HALF :] + b[HALF : 2 * HALF]
-        gr[n] = b[2 * HALF :].astype(gr.dtype)
-
-
-def attention(meta, q, k, v, gm, left, right, earlier, off, heads):
+        return cols, b, qb, gb, kc, vc, p.astype(BF16), (p * (dp - delta)).astype(BF16)
+
+    terms = {}
+
+    def gradients(cols, b, qb, gb, kc, vc, pb, ds):
+        at = slice(b * HALF, (b + 1) * HALF)
+        att[at, cols] = dot_nn(pb, vc).astype(att.dtype)
+        dq[at, cols] = (dot_nn(ds, kc) * scale).astype(dq.dtype)
+        terms[cols.start, b] = (dot_tn(ds, qb) * scale, dot_tn(pb, gb))
+
+    tasks = [
+        (slice(n * HEAD_DIM, (n + 1) * HEAD_DIM), b)
+        for n in range(q.shape[1] // HEAD_DIM)
+        for b in range(rows // HALF)
+    ]
+    ahead = products(*tasks[0])
+    behind = None
+    for n in range(len(tasks)):
+        now, ahead = ahead, products(*tasks[n + 1]) if n + 1 < len(tasks) else None
+        done = softmax(*now)
+        if behind is not None:
+            gradients(*behind)
+        behind = done
+    gradients(*behind)
+    for cols in dict.fromkeys(task[0].start for task in tasks):
+        for n, own in enumerate((dk, dv)):
+            a, b = terms[cols, 0][n], terms[cols, 1][n]
+            at = slice(cols, cols + HEAD_DIM)
+            gl[n, :, at] = a[0:HALF].astype(gl.dtype)
+            own[0:HALF, at] = a[HALF : 2 * HALF] + b[0:HALF]
+            own[HALF:, at] = a[2 * HALF :] + b[HALF : 2 * HALF]
+            gr[n, :, at] = b[2 * HALF :].astype(gr.dtype)
+
+
+def attention(meta, q, k, v, gm, left, right, earlier, off, heads, starts, group_heads):
     rows, width = q.shape
-
-    def at(n, o):
-        return pl.BlockSpec((n, HEAD_DIM), lambda h, s: (0, h + o))
-
-    pair = pl.BlockSpec((2, HALF, HEAD_DIM), lambda h, s: (0, 0, h))
-    w = heads * HEAD_DIM
-    aliases = {7: 0, 8: 1} if earlier else {}
+    wide = 2 * HEAD_DIM
+
+    def at(o):
+        return pl.BlockSpec((rows, wide), lambda h, s: (0, h + o // 2))
+
+    def pair(o):
+        return pl.BlockSpec((2, HALF, wide), lambda h, s: (0, 0, h + o // 2))
+
+    w = group_heads * HEAD_DIM
     return pl.pallas_call(
         attention_kernel,
         name="attention",
@@ -98,12 +123,12 @@
         ],
         grid_spec=pltpu.PrefetchScalarGridSpec(
             num_scalar_prefetch=1,
-            grid=(heads,),
-            in_specs=[at(rows, off)] * 4 + [pair] * 2 + [ANY] * len(earlier),
-            out_specs=[at(rows, off)] * 2 + [at(rows, 0)] * 2 + [pair] * 2,
+            grid=(heads // 2,),
+            in_specs=[at(off)] * 3 + [at(starts[0])] + [pair(0)] * 2 + [ANY] * len(earlier),
+            out_specs=[at(off)] * 2 + [at(starts[1])] * 2 + [pair(starts[1])] * 2,
             scratch_shapes=[pltpu.VMEM((rows // HALF, HALF, 3 * HALF), F32)],
         ),
-        input_output_aliases=aliases,
+        input_output_aliases={7 + n: n for n in range(len(earlier))},
         compiler_params=pltpu.CompilerParams(dimension_semantics=("arbitrary",)),
     )(meta, q, k, v, gm, left, right, *earlier)
 
@@ -224,16 +249,16 @@
 
 def mixed(place, go, pieces):
     rows, width = go.shape
-    whole = pl.BlockSpec((rows, width), lambda i, s: (0, 0))
+    cols = pieces[0].shape[-1]
     return pl.pallas_call(
         mixed_kernel,
         name="mixed",
-        out_shape=SDS((rows, width), BF16),
+        out_shape=SDS((rows, cols), BF16),
         grid_spec=pltpu.PrefetchScalarGridSpec(
             num_scalar_prefetch=1,
             grid=(1,),
-            in_specs=[whole] + [ANY] * 8,
-            out_specs=whole,
+            in_specs=[pl.BlockSpec((rows, width), lambda i, s: (0, 0))] + [ANY] * 8,
+            out_specs=pl.BlockSpec((rows, cols), lambda i, s: (0, 0)),
             scratch_shapes=[
                 pltpu.VMEM((4, 2, 2) + pieces[0].shape[1:], BF16),
                 pltpu.SemaphoreType.DMA((8,)),
@@ -246,23 +271,26 @@
     return lax.ppermute(value, "dp", [(i, i ^ bit) for i in range(lax.axis_size("dp"))])
 
 
-def gathered(shard):
+def gathered(shard, cuts):
     low = (lax.axis_index("dp") // 2) % 2 == 0
     other = swapped(shard, 2)
-    mine = [jnp.stack([jnp.where(low, shard, other), jnp.where(low, other, shard)])]
-    for n in (1, 2, 3):
-        mine.append(turned(mine[0], "dp", 4 * n))
-    theirs = []
-    for piece in mine:
-        theirs.append(swapped(piece, 1))
-    return mine + theirs
-
-
-def deal_kernel(z, *refs):
-    *ins, spread = refs
-    own, *outs = ins[-8:]
-    ins = ins[:-8]
-    n = own.shape[1]
+    groups = []
+    for a, b in cuts:
+        own, far = shard[:, a:b], other[:, a:b]
+        mine = [jnp.stack([jnp.where(low, own, far), jnp.where(low, far, own)])]
+        for n in (1, 2, 3):
+            mine.append(turned(mine[0], "dp", 4 * n))
+        theirs = []
+        for piece in mine:
+            theirs.append(swapped(piece, 1))
+        groups.append(mine + theirs)
+    return groups
+
+
+def deal_kernel(*refs):
+    *ins, out, spread = refs
+    count, rows, _ = out.shape
+    n = rows // 2
     off = 0
     for chunk in range(0, len(ins), 4):
         first, *rest = ins[chunk : chunk + 4]
@@ -271,58 +299,53 @@
             total = total + got[...].astype(F32)
         wide = total.shape[1]
         for x in range(2):
-            for k in range(8):
-                row = (x * 8 + k) * n
-                spread[x, k, 0:n, off : off + wide] = total[row : row + n]
+            for k in range(count):
+                row = (x * count + k) * n
+                spread[k, x * n : (x + 1) * n, off : off + wide] = total[row : row + n]
         off += wide
-    for k, out in enumerate((own, *outs)):
-        for x in range(2):
-            out[x] = spread[x, lax.rem(z[0] + k, 8), 0:n].astype(out.dtype)
-
-
-def deal(z, parts, width):
-    rows = parts[0].shape[0] // 16
-    shape = (2, rows, width)
+    out[...] = spread[...].astype(out.dtype)
+
+
+def deal(parts, count, width):
+    shape = (count, parts[0].shape[0] // count, width)
     return pl.pallas_call(
         deal_kernel,
         name="deal",
-        out_shape=[SDS(shape, F32)] + [SDS(shape, BF16)] * 7,
+        out_shape=SDS(shape, BF16),
+        grid=(1,),
+        in_specs=[pl.BlockSpec(p.shape, lambda i: (0, 0)) for p in parts],
+        out_specs=pl.BlockSpec(shape, lambda i: (0, 0, 0)),
+        scratch_shapes=[pltpu.VMEM(shape, F32)],
+    )(*parts)
+
+
+def quarter_kernel(place, got, *outs):
+    total = got[0].astype(F32)
+    for k in range(1, got.shape[0]):
+        total = total + got[k].astype(F32)
+    n = outs[0].shape[0]
+    quarters = [total[i * n : (i + 1) * n] for i in range(4)]
+    for k, out in enumerate(outs):
+        x, h = place[0] ^ (k // 2), place[1] ^ (k % 2)
+        low = jnp.where(h == 0, quarters[0], quarters[1])
+        high = jnp.where(h == 0, quarters[2], quarters[3])
+        out[...] = jnp.where(x == 0, low, high)
+
+
+def quartered(place, got):
+    _, rows, width = got.shape
+    part = pl.BlockSpec((rows // 4, width), lambda i, s: (0, 0))
+    return pl.pallas_call(
+        quarter_kernel,
+        name="quarter",
+        out_shape=[SDS((rows // 4, width), F32)] * 4,
         grid_spec=pltpu.PrefetchScalarGridSpec(
             num_scalar_prefetch=1,
             grid=(1,),
-            in_specs=[pl.BlockSpec(p.shape, lambda i, s: (0, 0)) for p in parts],
-            out_specs=[pl.BlockSpec(shape, lambda i, s: (0, 0, 0))] * 8,
-            scratch_shapes=[pltpu.VMEM((2, 8, 16, width), F32)],
+            in_specs=[pl.BlockSpec(got.shape, lambda i, s: (0, 0, 0))],
+            out_specs=[part] * 4,
         ),
-    )(z, *parts)
-
-
-def quarter_kernel(place, own, *refs):
-    gots, outs = refs[:7], refs[7:]
-    total = own[...]
-    for got in gots:
-        total = total + got[...].astype(F32)
-    n = outs[0].shape[0]
-    quarters = [[total[x, h * n : (h + 1) * n] for h in range(2)] for x in range(2)]
-    for k, out in enumerate(outs):
-        x, h = place[0] ^ (k // 2), place[1] ^ (k % 2)
-        low = jnp.where(h == 0, quarters[0][0], quarters[0][1])
-        high = jnp.where(h == 0, quarters[1][0], quarters[1][1])
-        out[...] = jnp.where(x == 0, low, high)
-
-
-def quartered(place, own, gots):
-    _, rows, width = own.shape
-    whole = pl.BlockSpec(own.shape, lambda i, s: (0, 0, 0))
-    part = pl.BlockSpec((rows // 2, width), lambda i, s: (0, 0))
-    return pl.pallas_call(
-        quarter_kernel,
-        name="quarter",
-        out_shape=[SDS((rows // 2, width), F32)] * 4,
-        grid_spec=pltpu.PrefetchScalarGridSpec(
-            num_scalar_prefetch=1, grid=(1,), in_specs=[whole] * 8, out_specs=[part] * 4
-        ),
-    )(place, own, *gots)
+    )(place, got)
 
 
 def crossed(value, k):
@@ -336,54 +359,66 @@
 
 
 CHUNKS = (8, 4)
+GROUPS = ((0,), (1,))
+MIXED = ((0, 1),)
 
 
 def step(queries, keys, values, grad_out, out_weight, lengths):
     rows, width = queries.shape
     first_row = lax.axis_index("seq") * rows
-    dp = lax.axis_index("dp")
+    dp, seq = lax.axis_index("dp"), lax.axis_index("seq")
     y, core = dp // 4, dp % 2
     meta = jnp.stack([first_row, lengths[0]]).astype(jnp.int32)
-    offs = [sum(CHUNKS[:n]) for n in range(len(CHUNKS))]
-    pieces = gathered(out_weight)
+    offs = [sum(CHUNKS[:n]) for n in range(len(CHUNKS) + 1)]
+    cuts = [(offs[m[0]] * HEAD_DIM, offs[m[-1] + 1] * HEAD_DIM) for m in MIXED]
+    weights = gathered(out_weight, cuts)
     halos = []
-    for off, heads in zip(offs, CHUNKS):
-        a, b = off * HEAD_DIM, (off + heads) * HEAD_DIM
+    for n in range(len(CHUNKS)):
+        a, b = offs[n] * HEAD_DIM, offs[n + 1] * HEAD_DIM
         tail = jnp.stack([keys[rows - HALF :, a:b], values[rows - HALF :, a:b]])
         head = jnp.stack([keys[:HALF, a:b], values[:HALF, a:b]])
         left = passed(tail, "seq", 1)
         right = passed(head, "seq", -1)
         halos.append((left, right))
-    grad_mixed = mixed(jnp.stack([y, core]).astype(jnp.int32), grad_out, pieces)
-    earlier, sums, parts = (), [], []
-    for (left, right), off, heads in zip(halos, offs, CHUNKS):
-        att, dq, dk, dv, gl, gr = attention(
-            meta, queries, keys, values, grad_mixed, left, right, earlier, off, heads
-        )
-        earlier = (att, dq)
+    mixes = {}
+    for g, chunks in enumerate(MIXED):
+        part = mixed(jnp.stack([y, core]).astype(jnp.int32), grad_out, weights[g])
+        for n in chunks:
+            mixes[n] = part, offs[n] - offs[chunks[0]]
+    whole, sums, parts = (), [], []
+    for chunks in GROUPS:
+        off, heads = offs[chunks[0]], sum(CHUNKS[n] for n in chunks)
+        terms = ()
+        for n in chunks:
+            part, start = mixes[n]
+            made = attention(
+                meta, queries, keys, values, part, *halos[n], whole + terms,
+                offs[n], CHUNKS[n], (start, offs[n] - off), heads,
+            )
+            whole, terms = tuple(made[:2]), tuple(made[2:])
+        dk, dv, gl, gr = terms
         low = passed(gr, "seq", 1)
         high = passed(gl, "seq", -1)
         sums.append((dk, dv, low, high))
-        keep, send = weight_parts(core[None], grad_out, att, off, heads)
+        keep, send = weight_parts(core[None], grad_out, whole[0], off, heads)
         got = swapped(send, 1)
         own, *rest = parted(y[None], keep, got)
         gots = []
         for k, part in enumerate(rest):
             gots.append(turned(part, "dp", 4 * (k + 1)))
         parts += [own, *gots]
-    seq = lax.axis_index("seq")
-    own, *rest = deal((seq // 2)[None], parts, width)
-    gots = []
-    for k, part in enumerate(rest):
-        gots.append(turned(part, "seq", 2 * (k + 1)))
+    count = lax.axis_size("seq")
+    dealt = deal(parts, count // 2, width)
+    rings = [list(range(k, count, 2)) for k in range(2)]
+    got = lax.all_to_all(dealt, "seq", 0, 0, tiled=True, axis_index_groups=rings)
     place = jnp.stack([(dp // 2) % 2, seq % 2]).astype(jnp.int32)
-    own, *rest = quartered(place, own, gots)
+    own, *rest = quartered(place, got)
     for k, part in enumerate(rest):
         own = own + crossed(part, k + 1)
     outs = ()
-    for n, off in enumerate(offs):
-        outs = tuple(join(*sums[n], outs, off * HEAD_DIM, width))
-    return dq, outs[0], outs[1], own
+    for g, chunks in enumerate(GROUPS):
+        outs = tuple(join(*sums[g], outs, offs[chunks[0]] * HEAD_DIM, width))
+    return whole[1], outs[0], outs[1], own
 
 
 def solution(mesh):

time: 273 us -> 255 us (0.934)
  the two profiles are of different devices: /device:TPU:18 before, /device:TPU:139 now
where the time goes in v3:
time: 255 us; the launch traced here: 254 us
  waiting for transfers between devices  114 us (45%)
  Pallas kernels  65.4 us (26%)
  starting transfers between devices  58.2 us (23%)
  local copies, waits for them, and re-layouts  9.59 us (4%)
  other arithmetic  5.74 us (2%)
    ppermute x8, waiting for transfers between devices, passed(): return lax.ppermute(value, axis, pairs)  56.8 us
    ppermute x9, waiting for transfers between devices, turned(): lax.ppermute(value, axis, [(i, (i + by) % devices) for i in range(devices)])  39.1 us
    ppermute x8, starting transfers between devices, passed(): return lax.ppermute(value, axis, pairs)  33.4 us
    pallas_call x2, Pallas kernels, attention(): pl.pallas_call(attention_kernel, name='attention', out_shape=[SDS((rows,...  25.8 us
    ppermute x9, starting transfers between devices, turned(): lax.ppermute(value, axis, [(i, (i + by) % devices) for i in range(devices)])  10.7 us
    pallas_call x2, Pallas kernels, weight_parts(): pl.pallas_call(weight_kernel, name='weight', out_shape=[SDS((4, width //...  10.6 us
    ppermute x7, waiting for transfers between devices, swapped(): lax.ppermute(value, 'dp', [(i, i ^ bit) for i in range(lax.axis_size('dp'...  9.98 us
    pallas_call x1, Pallas kernels, mixed(): pl.pallas_call(mixed_kernel, name='mixed', out_shape=SDS((rows, cols), BF...  8.19 us
  transfers between devices with their start and end apart: 28, of which 14 were waited for; matrix products, arithmetic and copies ran while one was open for 3% of the time, Pallas kernels for 17%

profile of v3, /device:TPU:139, one launch (start us, length us, event | category | flops | bytes accessed | tf_op | source)
XLA Modules:
  0.0 254.2 jit_solution(2121150165414225041)
XLA Ops:
  1.0 7.8 %collective-permute-done = bf16[96,1536]{1,0:T(8,128)(2,1)S(1)} collective-permute-done((bf16[96,1536]{1,0:T(8,128)(2,1)}, bf16[96,1536]{1,0:T(8,128)(2,1)S(1)}, u32[]{:S(2)}, u32[]{:S(2)}) %collective-permute-start) | collective-permute-done | bytes 294944 | tf_op jit(solution)/shard_map/ppermute | solution.py:271
  14.0 3.7 %collective-permute-start.10 = (bf16[2,256,1024]{2,1,0:T(8,128)(2,1)}, bf16[2,256,1024]{2,1,0:T(8,128)(2,1)S(1)}, u32[]{:S(2)}, u32[]{:S(2)}) collective-permute-start(bf16[2,256,1024]{2,1,0:T(8,128)(2,1)} %pad_maximum_fusion), channel_id=1, source_target_pairs={{0,1},{1,2},{2,3},{3,4},{4,5},{5,6},{6,7},{7,8},{8,9},{9,10},{10,1... | collective-permute-start | bytes 3145736 | tf_op jit(solution)/shard_map/ppermute | solution.py:224
  23.0 5.1 %collective-permute-start.11 = (bf16[2,256,1024]{2,1,0:T(8,128)(2,1)}, bf16[2,256,1024]{2,1,0:T(8,128)(2,1)}, u32[]{:S(2)}, u32[]{:S(2)}) collective-permute-start(bf16[2,256,1024]{2,1,0:T(8,128)(2,1)} %pad_maximum_fusion.1), channel_id=1, source_target_pairs={{1,0},{2,1},{3,2},{4,3},{5,4},{6,5},{7,6},{8,7},{9,8},{10,9},{11,1... | collective-permute-start | bytes 3145736 | tf_op jit(solution)/shard_map/ppermute | solution.py:224
  28.1 4.3 %collective-permute-done.3.refs_3_ = bf16[2,96,1536]{2,1,0:T(8,128)(2,1)} collective-permute-done((bf16[2,96,1536]{2,1,0:T(8,128)(2,1)S(1)}, bf16[2,96,1536]{2,1,0:T(8,128)(2,1)}, u32[]{:S(2)}, u32[]{:S(2)}) %collective-permute-start.3) | collective-permute-done | bytes 589856 | tf_op jit(solution)/shard_map/ppermute | solution.py:229
  33.7 12.4 %collective-permute-done.2.refs_2_ = bf16[2,96,1536]{2,1,0:T(8,128)(2,1)} collective-permute-done((bf16[2,96,1536]{2,1,0:T(8,128)(2,1)S(1)}, bf16[2,96,1536]{2,1,0:T(8,128)(2,1)}, u32[]{:S(2)}, u32[]{:S(2)}) %collective-permute-start.2) | collective-permute-done | bytes 589856 | tf_op jit(solution)/shard_map/ppermute | solution.py:229
  51.9 8.2 %mixed.1.gm = bf16[512,1536]{1,0:T(8,128)(2,1)} custom-call(s32[2]{0:T(128)} %pad_add_fusion.1.place, bf16[512,1536]{1,0:T(8,128)(2,1)} %go.5, bf16[2,96,1536]{2,1,0:T(8,128)(2,1)} %copy-done.2, bf16[2,96,1536]{2,1,0:T(8,128)(2,1)} %collective-permute-done.1.refs_1_, bf16[2,96,1536]{2,1,0:T(8,128)(2,1)} %collective-permute-done.2.refs_2_, ...), custom_call_target="tpu_custom_call" | custom-call | tf_op jit(solution)/shard_map/mixed/pallas_call | solution.py:253
  62.9 4.5 %collective-permute-done.11.right = bf16[2,256,1024]{2,1,0:T(8,128)(2,1)} collective-permute-done((bf16[2,256,1024]{2,1,0:T(8,128)(2,1)}, bf16[2,256,1024]{2,1,0:T(8,128)(2,1)}, u32[]{:S(2)}, u32[]{:S(2)}) %collective-permute-start.11) | collective-permute-done | bytes 1048608 | tf_op jit(solution)/shard_map/ppermute | solution.py:224
  67.4 16.1 %attention.2 = (bf16[512,1536]{1,0:T(8,128)(2,1)}, bf16[512,1536]{1,0:T(8,128)(2,1)}, f32[512,1024]{1,0:T(8,128)}, f32[512,1024]{1,0:T(8,128)}, bf16[2,256,1024]...) custom-call(s32[2]{0:T(128)} %pad_add_fusion.meta, bf16[512,1536]{1,0:T(8,128)(2,1)} %q.3, bf16[512,1536]{1,0:T(8,128)(2,1)} %k.3, ...), custom_call_target="tpu_custom_call" | custom-call | tf_op jit(solution)/shard_map/attention/pallas_call | solution.py:113
  83.5 5.9 %weight.2 = (f32[4,192,1024]{2,1,0:T(8,128)}, bf16[4,192,1024]{2,1,0:T(8,128)(2,1)}) custom-call(s32[1]{0:T(128)} %bitcast.2.core, bf16[512,1536]{1,0:T(8,128)(2,1)} %go.5, bf16[512,1536]{1,0:T(8,128)(2,1)} %get-tuple-element.36.refs_0_.att), custom_call_target="tpu_custom_call" | custom-call | tf_op jit(solution)/shard_map/weight/pallas_call | solution.py:172
  92.7 6.5 %collective-permute-start.9 = (bf16[2,256,512]{2,1,0:T(8,128)(2,1)S(1)}, bf16[2,256,512]{2,1,0:T(8,128)(2,1)S(1)}, u32[]{:S(2)}, u32[]{:S(2)}) collective-permute-start(bf16[2,256,512]{2,1,0:T(8,128)(2,1)S(1)} %pad_maximum_fusion.4), channel_id=1, source_target_pairs={{1,0},{2,1},{3,2},{4,3},{5,4},{6,5},{7,6},{8,7},{9,8},{10,9},{11,1... | collective-permute-start | bytes 1572872 | tf_op jit(solution)/shard_map/ppermute | solution.py:224
  99.1 15.9 %collective-permute-done.8.left = bf16[2,256,512]{2,1,0:T(8,128)(2,1)S(1)} collective-permute-done((bf16[2,256,512]{2,1,0:T(8,128)(2,1)S(1)}, bf16[2,256,512]{2,1,0:T(8,128)(2,1)S(1)}, u32[]{:S(2)}, u32[]{:S(2)}) %collective-permute-start.8) | collective-permute-done | bytes 524320 | tf_op jit(solution)/shard_map/ppermute | solution.py:224
  115.1 5.5 %collective-permute-done.9.right = bf16[2,256,512]{2,1,0:T(8,128)(2,1)S(1)} collective-permute-done((bf16[2,256,512]{2,1,0:T(8,128)(2,1)S(1)}, bf16[2,256,512]{2,1,0:T(8,128)(2,1)S(1)}, u32[]{:S(2)}, u32[]{:S(2)}) %collective-permute-start.9) | collective-permute-done | bytes 524320 | tf_op jit(solution)/shard_map/ppermute | solution.py:224
  121.4 9.7 %attention.3 = (bf16[512,1536]{1,0:T(8,128)(2,1)}, bf16[512,1536]{1,0:T(8,128)(2,1)}, f32[512,512]{1,0:T(8,128)}, f32[512,512]{1,0:T(8,128)}, bf16[2,256,512]{2,...) custom-call(s32[2]{0:T(128)} %pad_add_fusion.meta, bf16[512,1536]{1,0:T(8,128)(2,1)} %q.3, ...), custom_call_target="tpu_custom_call", output_to_operand_aliasing={{0}: (7, {}), {1}: (8, {})} | custom-call | tf_op jit(solution)/shard_map/attention/pallas_call | solution.py:113
  131.1 4.7 %weight.3 = (f32[4,192,512]{2,1,0:T(8,128)}, bf16[4,192,512]{2,1,0:T(8,128)(2,1)}) custom-call(s32[1]{0:T(128)} %bitcast.2.core, bf16[512,1536]{1,0:T(8,128)(2,1)} %go.5, bf16[512,1536]{1,0:T(8,128)(2,1)} %get-tuple-element.57.att), custom_call_target="tpu_custom_call" | custom-call | tf_op jit(solution)/shard_map/weight/pallas_call | solution.py:172
  145.2 4.5 %parted.2 = (f32[192,1024]{1,0:T(8,128)}, bf16[192,1024]{1,0:T(8,128)(2,1)}, bf16[192,1024]{1,0:T(8,128)(2,1)}, bf16[192,1024]{1,0:T(8,128)(2,1)}) custom-call(s32[1]{0:T(128)} %bitcast.1.y, f32[4,192,1024]{2,1,0:T(8,128)} %get-tuple-element.51.keep, bf16[4,192,1024]{2,1,0:T(8,128)(2,1)} %copy-done.3), custom_call_target="tpu_custom_call" | custom-call | tf_op jit(solution)/shard_map/parted/pallas_call | solution.py:208
  154.9 20.0 %collective-permute-done.22.refs_6_ = bf16[192,512]{1,0:T(8,128)(2,1)S(1)} collective-permute-done((bf16[192,512]{1,0:T(8,128)(2,1)}, bf16[192,512]{1,0:T(8,128)(2,1)S(1)}, u32[]{:S(2)}, u32[]{:S(2)}) %collective-permute-start.22) | collective-permute-done | bytes 196640 | tf_op jit(solution)/shard_map/ppermute | solution.py:229
  179.9 4.6 %collective-permute-start.15 = (bf16[2,256,1024]{2,1,0:T(8,128)(2,1)}, bf16[2,256,1024]{2,1,0:T(8,128)(2,1)S(1)}, u32[]{:S(2)}, u32[]{:S(2)}) collective-permute-start(bf16[2,256,1024]{2,1,0:T(8,128)(2,1)} %get-tuple-element.46), channel_id=1, source_target_pairs={{1,0},{2,1},{3,2},{4,3},{5,4},{6,5},{7,6},{8,7},{9,8},{10,9},{11,1... | collective-permute-start | bytes 3145736 | tf_op jit(solution)/shard_map/ppermute | solution.py:224
  188.6 6.6 %all-to-all-start = ((bf16[8,24,1536]{2,1,0:T(8,128)(2,1)}), bf16[8,24,1536]{2,1,0:T(8,128)(2,1)S(1)}, u32[]{:S(2)}, u32[]{:S(2)}) async-start(bf16[8,24,1536]{2,1,0:T(8,128)(2,1)} %deal.1), calls=%async_computation | async-start | bytes 1179648 | tf_op jit(solution)/shard_map/all_to_all | solution.py:413
  197.4 6.8 %collective-permute-start.13 = (bf16[2,256,512]{2,1,0:T(8,128)(2,1)}, bf16[2,256,512]{2,1,0:T(8,128)(2,1)}, u32[]{:S(2)}, u32[]{:S(2)}) collective-permute-start(bf16[2,256,512]{2,1,0:T(8,128)(2,1)} %get-tuple-element.42), channel_id=1, source_target_pairs={{1,0},{2,1},{3,2},{4,3},{5,4},{6,5},{7,6},{8,7},{9,8},{10,9},{11,1... | collective-permute-start | bytes 1572872 | tf_op jit(solution)/shard_map/ppermute | solution.py:224
  204.7 7.8 %all-to-all-done.got = bf16[8,24,1536]{2,1,0:T(8,128)(2,1)S(1)} async-done(((bf16[8,24,1536]{2,1,0:T(8,128)(2,1)}), bf16[8,24,1536]{2,1,0:T(8,128)(2,1)S(1)}, u32[]{:S(2)}, u32[]{:S(2)}) %all-to-all-start) | async-done | bytes 589856 | tf_op jit(solution)/shard_map/all_to_all | solution.py:413
  216.8 13.7 %collective-permute-done.14.low = bf16[2,256,1024]{2,1,0:T(8,128)(2,1)S(1)} collective-permute-done((bf16[2,256,1024]{2,1,0:T(8,128)(2,1)}, bf16[2,256,1024]{2,1,0:T(8,128)(2,1)S(1)}, u32[]{:S(2)}, u32[]{:S(2)}) %collective-permute-start.14) | collective-permute-done | bytes 1048608 | tf_op jit(solution)/shard_map/ppermute | solution.py:224
  230.8 8.6 %collective-permute-done.15.high = bf16[2,256,1024]{2,1,0:T(8,128)(2,1)S(1)} collective-permute-done((bf16[2,256,1024]{2,1,0:T(8,128)(2,1)}, bf16[2,256,1024]{2,1,0:T(8,128)(2,1)S(1)}, u32[]{:S(2)}, u32[]{:S(2)}) %collective-permute-start.15) | collective-permute-done | bytes 1048608 | tf_op jit(solution)/shard_map/ppermute | solution.py:224
  240.4 4.6 %join.2 = (bf16[512,1536]{1,0:T(8,128)(2,1)}, bf16[512,1536]{1,0:T(8,128)(2,1)}) custom-call(f32[512,1024]{1,0:T(8,128)} %get-tuple-element.43.dk, f32[512,1024]{1,0:T(8,128)} %get-tuple-element.44.dv, bf16[2,256,1024]{2,1,0:T(8,128)(2,1)} %copy-done.5, bf16[2,256,1024]{2,1,0:T(8,128)(2,1)} %copy-done.6), custom_call_target="tpu_custom_call" | custom-call | tf_op jit(solution)/shard_map/join/pallas_call | solution.py:147
  245.0 5.8 %collective-permute-done.13.high = bf16[2,256,512]{2,1,0:T(8,128)(2,1)} collective-permute-done((bf16[2,256,512]{2,1,0:T(8,128)(2,1)}, bf16[2,256,512]{2,1,0:T(8,128)(2,1)}, u32[]{:S(2)}, u32[]{:S(2)}) %collective-permute-start.13) | collective-permute-done | bytes 524320 | tf_op jit(solution)/shard_map/ppermute | solution.py:224
  (95 shorter events, 59.2 us)
Async XLA Ops:
  9.9 13.1 %collective-permute-start.4 = (bf16[2,96,1536]{2,1,0:T(8,128)(2,1)S(1)}, bf16[2,96,1536]{2,1,0:T(8,128)(2,1)S(1)}, u32[]{:S(2)}, u32[]{:S(2)}) collective-permute-start(bf16[2,96,1536]{2,1,0:T(8,128)(2,1)S(1)} %pad_maximum_fusion.2.refs_0_), channel_id=1, source_target_pairs={{0,16},{16,0},{32,48},{48,32},{64,80},{80,64},{96,112},{112,96},{1... | collective-permute-start | bytes 1769480 | tf_op jit(solution)/shard_map/ppermute | solution.py:271
  14.0 48.9 %collective-permute-start.10 = (bf16[2,256,1024]{2,1,0:T(8,128)(2,1)}, bf16[2,256,1024]{2,1,0:T(8,128)(2,1)S(1)}, u32[]{:S(2)}, u32[]{:S(2)}) collective-permute-start(bf16[2,256,1024]{2,1,0:T(8,128)(2,1)} %pad_maximum_fusion), channel_id=1, source_target_pairs={{0,1},{1,2},{2,3},{3,4},{4,5},{5,6},{6,7},{7,8},{8,9},{9,10},{10,1... | collective-permute-start | bytes 3145736 | tf_op jit(solution)/shard_map/ppermute | solution.py:224
  17.8 14.7 %collective-permute-start.3 = (bf16[2,96,1536]{2,1,0:T(8,128)(2,1)S(1)}, bf16[2,96,1536]{2,1,0:T(8,128)(2,1)}, u32[]{:S(2)}, u32[]{:S(2)}) collective-permute-start(bf16[2,96,1536]{2,1,0:T(8,128)(2,1)S(1)} %pad_maximum_fusion.2.refs_0_), channel_id=1, source_target_pairs={{0,192},{16,208},{32,224},{48,240},{64,0},{80,16},{96,32},{112,48}... | collective-permute-start | bytes 1769480 | tf_op jit(solution)/shard_map/ppermute | solution.py:229
  18.0 28.1 %collective-permute-start.2 = (bf16[2,96,1536]{2,1,0:T(8,128)(2,1)S(1)}, bf16[2,96,1536]{2,1,0:T(8,128)(2,1)}, u32[]{:S(2)}, u32[]{:S(2)}) collective-permute-start(bf16[2,96,1536]{2,1,0:T(8,128)(2,1)S(1)} %pad_maximum_fusion.2.refs_0_), channel_id=1, source_target_pairs={{0,128},{16,144},{32,160},{48,176},{64,192},{80,208},{96,224},{112... | collective-permute-start | bytes 1769480 | tf_op jit(solution)/shard_map/ppermute | solution.py:229
  20.3 27.0 %collective-permute-start.1 = (bf16[2,96,1536]{2,1,0:T(8,128)(2,1)S(1)}, bf16[2,96,1536]{2,1,0:T(8,128)(2,1)}, u32[]{:S(2)}, u32[]{:S(2)}) collective-permute-start(bf16[2,96,1536]{2,1,0:T(8,128)(2,1)S(1)} %pad_maximum_fusion.2.refs_0_), channel_id=1, source_target_pairs={{0,64},{16,80},{32,96},{48,112},{64,128},{80,144},{96,160},{112,17... | collective-permute-start | bytes 1769480 | tf_op jit(solution)/shard_map/ppermute | solution.py:229
  23.0 44.4 %collective-permute-start.11 = (bf16[2,256,1024]{2,1,0:T(8,128)(2,1)}, bf16[2,256,1024]{2,1,0:T(8,128)(2,1)}, u32[]{:S(2)}, u32[]{:S(2)}) collective-permute-start(bf16[2,256,1024]{2,1,0:T(8,128)(2,1)} %pad_maximum_fusion.1), channel_id=1, source_target_pairs={{1,0},{2,1},{3,2},{4,3},{5,4},{6,5},{7,6},{8,7},{9,8},{10,9},{11,1... | collective-permute-start | bytes 3145736 | tf_op jit(solution)/shard_map/ppermute | solution.py:224
  32.4 19.5 %collective-permute-start.7 = (bf16[2,96,1536]{2,1,0:T(8,128)(2,1)}, bf16[2,96,1536]{2,1,0:T(8,128)(2,1)}, u32[]{:S(2)}, u32[]{:S(2)}) collective-permute-start(bf16[2,96,1536]{2,1,0:T(8,128)(2,1)} %collective-permute-done.3.refs_3_), channel_id=1, source_target_pairs={{0,16},{16,0},{32,48},{48,32},{64,80},{80,64},{96,112},{112,96},{1... | collective-permute-start | bytes 1769480 | tf_op jit(solution)/shard_map/ppermute | solution.py:271
  89.4 54.6 %collective-permute-start.16 = (bf16[4,192,1024]{2,1,0:T(8,128)(2,1)}, bf16[4,192,1024]{2,1,0:T(8,128)(2,1)S(1)}, u32[]{:S(2)}, u32[]{:S(2)}) collective-permute-start(bf16[4,192,1024]{2,1,0:T(8,128)(2,1)} %get-tuple-element.52), channel_id=1, source_target_pairs={{0,16},{16,0},{32,48},{48,32},{64,80},{80,64},{96,112},{112,96},{1... | collective-permute-start | bytes 4718600 | tf_op jit(solution)/shard_map/ppermute | solution.py:271
  90.0 25.1 %collective-permute-start.8 = (bf16[2,256,512]{2,1,0:T(8,128)(2,1)S(1)}, bf16[2,256,512]{2,1,0:T(8,128)(2,1)S(1)}, u32[]{:S(2)}, u32[]{:S(2)}) collective-permute-start(bf16[2,256,512]{2,1,0:T(8,128)(2,1)S(1)} %pad_maximum_fusion.3), channel_id=1, source_target_pairs={{0,1},{1,2},{2,3},{3,4},{4,5},{5,6},{6,7},{7,8},{8,9},{9,10},{10,1... | collective-permute-start | bytes 1572872 | tf_op jit(solution)/shard_map/ppermute | solution.py:224
  92.7 27.9 %collective-permute-start.9 = (bf16[2,256,512]{2,1,0:T(8,128)(2,1)S(1)}, bf16[2,256,512]{2,1,0:T(8,128)(2,1)S(1)}, u32[]{:S(2)}, u32[]{:S(2)}) collective-permute-start(bf16[2,256,512]{2,1,0:T(8,128)(2,1)S(1)} %pad_maximum_fusion.4), channel_id=1, source_target_pairs={{1,0},{2,1},{3,2},{4,3},{5,4},{6,5},{7,6},{8,7},{9,8},{10,9},{11,1... | collective-permute-start | bytes 1572872 | tf_op jit(solution)/shard_map/ppermute | solution.py:224
  142.8 10.9 %collective-permute-start.21 = (bf16[192,512]{1,0:T(8,128)(2,1)}, bf16[192,512]{1,0:T(8,128)(2,1)S(1)}, u32[]{:S(2)}, u32[]{:S(2)}) collective-permute-start(bf16[192,512]{1,0:T(8,128)(2,1)} %get-tuple-element.61), channel_id=1, source_target_pairs={{0,64},{16,80},{32,96},{48,112},{64,128},{80,144},{96,160},{112,17... | collective-permute-start | bytes 589832 | tf_op jit(solution)/shard_map/ppermute | solution.py:229
  149.7 34.8 %collective-permute-start.17 = (bf16[192,1024]{1,0:T(8,128)(2,1)}, bf16[192,1024]{1,0:T(8,128)(2,1)S(1)}, u32[]{:S(2)}, u32[]{:S(2)}) collective-permute-start(bf16[192,1024]{1,0:T(8,128)(2,1)} %get-tuple-element.54), channel_id=1, source_target_pairs={{0,64},{16,80},{32,96},{48,112},{64,128},{80,144},{96,160},{112,17... | collective-permute-start | bytes 1179656 | tf_op jit(solution)/shard_map/ppermute | solution.py:229
  150.7 33.8 %collective-permute-start.18 = (bf16[192,1024]{1,0:T(8,128)(2,1)}, bf16[192,1024]{1,0:T(8,128)(2,1)S(1)}, u32[]{:S(2)}, u32[]{:S(2)}) collective-permute-start(bf16[192,1024]{1,0:T(8,128)(2,1)} %get-tuple-element.55), channel_id=1, source_target_pairs={{0,128},{16,144},{32,160},{48,176},{64,192},{80,208},{96,224},{112... | collective-permute-start | bytes 1179656 | tf_op jit(solution)/shard_map/ppermute | solution.py:229
  151.6 32.9 %collective-permute-start.19 = (bf16[192,1024]{1,0:T(8,128)(2,1)}, bf16[192,1024]{1,0:T(8,128)(2,1)S(1)}, u32[]{:S(2)}, u32[]{:S(2)}) collective-permute-start(bf16[192,1024]{1,0:T(8,128)(2,1)} %get-tuple-element.56), channel_id=1, source_target_pairs={{0,192},{16,208},{32,224},{48,240},{64,0},{80,16},{96,32},{112,48}... | collective-permute-start | bytes 1179656 | tf_op jit(solution)/shard_map/ppermute | solution.py:229
  152.5 22.4 %collective-permute-start.22 = (bf16[192,512]{1,0:T(8,128)(2,1)}, bf16[192,512]{1,0:T(8,128)(2,1)S(1)}, u32[]{:S(2)}, u32[]{:S(2)}) collective-permute-start(bf16[192,512]{1,0:T(8,128)(2,1)} %get-tuple-element.62), channel_id=1, source_target_pairs={{0,128},{16,144},{32,160},{48,176},{64,192},{80,208},{96,224},{112... | collective-permute-start | bytes 589832 | tf_op jit(solution)/shard_map/ppermute | solution.py:229
  153.7 25.5 %collective-permute-start.23 = (bf16[192,512]{1,0:T(8,128)(2,1)}, bf16[192,512]{1,0:T(8,128)(2,1)S(1)}, u32[]{:S(2)}, u32[]{:S(2)}) collective-permute-start(bf16[192,512]{1,0:T(8,128)(2,1)} %get-tuple-element.63), channel_id=1, source_target_pairs={{0,192},{16,208},{32,224},{48,240},{64,0},{80,16},{96,32},{112,48}... | collective-permute-start | bytes 589832 | tf_op jit(solution)/shard_map/ppermute | solution.py:229
  174.9 55.6 %collective-permute-start.14 = (bf16[2,256,1024]{2,1,0:T(8,128)(2,1)}, bf16[2,256,1024]{2,1,0:T(8,128)(2,1)S(1)}, u32[]{:S(2)}, u32[]{:S(2)}) collective-permute-start(bf16[2,256,1024]{2,1,0:T(8,128)(2,1)} %get-tuple-element.45), channel_id=1, source_target_pairs={{0,1},{1,2},{2,3},{3,4},{4,5},{5,6},{6,7},{7,8},{8,9},{9,10},{10,1... | collective-permute-start | bytes 3145736 | tf_op jit(solution)/shard_map/ppermute | solution.py:224
  179.9 59.6 %collective-permute-start.15 = (bf16[2,256,1024]{2,1,0:T(8,128)(2,1)}, bf16[2,256,1024]{2,1,0:T(8,128)(2,1)S(1)}, u32[]{:S(2)}, u32[]{:S(2)}) collective-permute-start(bf16[2,256,1024]{2,1,0:T(8,128)(2,1)} %get-tuple-element.46), channel_id=1, source_target_pairs={{1,0},{2,1},{3,2},{4,3},{5,4},{6,5},{7,6},{8,7},{9,8},{10,9},{11,1... | collective-permute-start | bytes 3145736 | tf_op jit(solution)/shard_map/ppermute | solution.py:224
  188.6 23.9 %all-to-all-start = ((bf16[8,24,1536]{2,1,0:T(8,128)(2,1)}), bf16[8,24,1536]{2,1,0:T(8,128)(2,1)S(1)}, u32[]{:S(2)}, u32[]{:S(2)}) async-start(bf16[8,24,1536]{2,1,0:T(8,128)(2,1)} %deal.1), calls=%async_computation | async-start | bytes 1179648 | tf_op jit(solution)/shard_map/all_to_all | solution.py:413
  195.2 49.8 %collective-permute-start.12 = (bf16[2,256,512]{2,1,0:T(8,128)(2,1)}, bf16[2,256,512]{2,1,0:T(8,128)(2,1)S(1)}, u32[]{:S(2)}, u32[]{:S(2)}) collective-permute-start(bf16[2,256,512]{2,1,0:T(8,128)(2,1)} %get-tuple-element.41), channel_id=1, source_target_pairs={{0,1},{1,2},{2,3},{3,4},{4,5},{5,6},{6,7},{7,8},{8,9},{9,10},{10,1... | collective-permute-start | bytes 1572872 | tf_op jit(solution)/shard_map/ppermute | solution.py:224
  197.4 53.4 %collective-permute-start.13 = (bf16[2,256,512]{2,1,0:T(8,128)(2,1)}, bf16[2,256,512]{2,1,0:T(8,128)(2,1)}, u32[]{:S(2)}, u32[]{:S(2)}) collective-permute-start(bf16[2,256,512]{2,1,0:T(8,128)(2,1)} %get-tuple-element.42), channel_id=1, source_target_pairs={{1,0},{2,1},{3,2},{4,3},{5,4},{6,5},{7,6},{8,7},{9,8},{10,9},{11,1... | collective-permute-start | bytes 1572872 | tf_op jit(solution)/shard_map/ppermute | solution.py:224
  215.8 37.7 %collective-permute-start.24 = (f32[6,1536]{1,0:T(8,128)}, f32[6,1536]{1,0:T(8,128)S(1)}, u32[]{:S(2)}, u32[]{:S(2)}) collective-permute-start(f32[6,1536]{1,0:T(8,128)} %get-tuple-element.65), channel_id=1, source_target_pairs={{0,1},{1,0},{2,3},{3,2},{4,5},{5,4},{6,7},{7,6},{8,9},{9,8},{10,11... | collective-permute-start | bytes 110600 | tf_op jit(solution)/shard_map/ppermute | solution.py:358
  230.6 23.0 %collective-permute-start.25 = (f32[6,1536]{1,0:T(8,128)}, f32[6,1536]{1,0:T(8,128)S(1)}, u32[]{:S(2)}, u32[]{:S(2)}) collective-permute-start(f32[6,1536]{1,0:T(8,128)} %get-tuple-element.66), channel_id=1, source_target_pairs={{0,32},{1,33},{2,34},{3,35},{4,36},{5,37},{6,38},{7,39},{8,40},{9,... | collective-permute-start | bytes 110600 | tf_op jit(solution)/shard_map/ppermute | solution.py:358
  239.4 14.1 %collective-permute-start.26 = (f32[6,1536]{1,0:T(8,128)}, f32[6,1536]{1,0:T(8,128)S(1)}, u32[]{:S(2)}, u32[]{:S(2)}) collective-permute-start(f32[6,1536]{1,0:T(8,128)} %get-tuple-element.67), channel_id=1, source_target_pairs={{0,33},{1,32},{2,35},{3,34},{4,37},{5,36},{6,39},{7,38},{8,41},{9,... | collective-permute-start | bytes 110600 | tf_op jit(solution)/shard_map/ppermute | solution.py:358
  (24 other events, 139.5 us)
